TPU v7x, 512 devices: a whole 4x8x8 slice. The times are simulated.
512 devices in a mesh: dp: 8 (over x, core), ctx: 64 (over z, y).
Axes of the slice: x: 4, y: 8, z: 8, core: 2. Of those that a mesh axis runs over, the one named last changes fastest.
Arguments:
- queries: bfloat16 [65536, 8192], P(('dp', 'ctx')), parts along dimension 0, may hold values from -6 to 6
- keys: bfloat16 [65536, 1024], P(('dp', 'ctx')), parts along dimension 0, may hold values from -6 to 6
- values: bfloat16 [65536, 1024], P(('dp', 'ctx')), parts along dimension 0, may hold values from -6 to 6
- order: int32 [65536], P('dp'), parts along dimension 0, may hold values from 0 to 8191, each once
- doc_lengths: int32 [128], P('dp'), parts along dimension 0, may hold values from 1 to 1024, 8192 in all
Outputs:
- attended: bfloat16 [65536, 8192], P(('dp', 'ctx')), parts along dimension 0
There are 8 independent parts, one for each index of `dp`. A program takes and returns all parts, laid end to end along the dimension named above; each array names one. Nothing has to cross between parts.
Inputs may be any that keep to these rules, and one draw needn't show every extreme that they name: `order`: each position of the packed sequence stands in exactly one slot. `doc_lengths`: the lengths sum to 8192; the largest is exactly 1024.
All inputs are finite; a program needn't handle non-finite values.
Results may differ from a plain program's by a relative error of at most 0.0046.
Values may be sent and summed in bfloat16 or wider, within the bound.
A program may use at most 128 MiB of HBM per device.

v0:
```python
import functools

import jax
import jax.numpy as jnp
from jax import lax
from jax.experimental import pallas as pl
from jax.sharding import Mesh
from jax.sharding import PartitionSpec as P

HEADS = 64
KV_HEADS = 8
HEAD_DIM = 128
BLOCK = 512


def document_starts(doc_lengths, tokens):
    doc_count = doc_lengths.shape[0]
    doc_ends = jnp.cumsum(doc_lengths)
    positions = jnp.arange(tokens, dtype=jnp.int32)
    doc_index = jnp.sum((positions[:, None] >= doc_ends[None, :]).astype(jnp.int32), axis=1)
    doc_firsts = doc_ends - doc_lengths
    matches = doc_index[:, None] == jnp.arange(doc_count, dtype=jnp.int32)[None, :]
    return jnp.sum(jnp.where(matches, doc_firsts[None, :], 0), axis=1)


def attn_kernel(doc_most, q_ref, k_ref, v_ref, ds_ref, o_ref):
    b = pl.program_id(0)
    window = doc_most + BLOCK
    start = pl.multiple_of(jnp.maximum(b * BLOCK - doc_most, 0), BLOCK)
    q = q_ref[...]
    k = k_ref[pl.ds(start, window), :]
    v = v_ref[pl.ds(start, window), :]
    s = lax.dot_general(q, k, (((1,), (1,)), ((), ())), preferred_element_type=jnp.float32)
    s = s * (HEAD_DIM ** (-0.5))
    qpos = b * BLOCK + lax.broadcasted_iota(jnp.int32, (BLOCK, window), 0)
    kpos = start + lax.broadcasted_iota(jnp.int32, (BLOCK, window), 1)
    visible = (kpos <= qpos) & (kpos >= ds_ref[...])
    s = jnp.where(visible, s, -jnp.inf)
    m = jnp.max(s, axis=1, keepdims=True)
    e = jnp.exp(s - m)
    l = jnp.sum(e, axis=1, keepdims=True)
    w = (e / l).astype(jnp.bfloat16)
    o_ref[...] = jnp.dot(w, v, preferred_element_type=jnp.float32).astype(o_ref.dtype)

def attend(q, k, v, doc_start, doc_most):
    tokens = q.shape[0]
    return pl.pallas_call(
        functools.partial(attn_kernel, doc_most),
        grid=(tokens // BLOCK,),
        in_specs=[
            pl.BlockSpec((BLOCK, HEAD_DIM), lambda b: (b, 0)),
            pl.BlockSpec((tokens, HEAD_DIM), lambda b: (0, 0)),
            pl.BlockSpec((tokens, HEAD_DIM), lambda b: (0, 0)),
            pl.BlockSpec((BLOCK, 1), lambda b: (b, 0)),
        ],
        out_specs=pl.BlockSpec((BLOCK, HEAD_DIM), lambda b: (b, 0)),
        out_shape=jax.ShapeDtypeStruct((tokens, HEAD_DIM), jnp.bfloat16),
    )(q, k, v, doc_start.reshape(tokens, 1))


def per_device(queries, keys, values, order, doc_lengths):
    nz = lax.axis_size("z")
    ny = lax.axis_size("y")
    tok_rows = queries.shape[0]
    tokens = tok_rows * nz * ny
    query_split = queries.reshape(tok_rows, HEADS, HEAD_DIM)
    query_heads = lax.all_to_all(query_split, ("z", "y"), split_axis=1, concat_axis=0, tiled=True)
    q_slots = query_heads.reshape(nz, ny, tok_rows, HEAD_DIM)
    q_ring = jnp.transpose(q_slots, (1, 0, 2, 3)).reshape(tokens, HEAD_DIM)
    paired = jnp.stack(
        [keys.reshape(tok_rows, KV_HEADS, HEAD_DIM), values.reshape(tok_rows, KV_HEADS, HEAD_DIM)],
        axis=2,
    )
    kv_col = lax.all_to_all(paired, "z", split_axis=1, concat_axis=0, tiled=True)
    kv_ring = lax.all_gather(kv_col, "y", axis=0, tiled=True).reshape(tokens, 2 * HEAD_DIM)
    joined = jnp.concatenate([q_ring, kv_ring], axis=1)
    doc_most = tokens // 8
    slot_ids = jnp.arange(tokens, dtype=jnp.int32)
    _, slot_of = lax.sort((order, slot_ids), num_keys=1)
    slot_dev = slot_of // tok_rows
    ring_row = (slot_dev % ny) * (nz * tok_rows) + (slot_dev // ny) * tok_rows + slot_of % tok_rows
    pos_rows = joined.at[ring_row].get(mode="promise_in_bounds", unique_indices=True)
    q_pos = pos_rows[:, :HEAD_DIM]
    k_pos = pos_rows[:, HEAD_DIM : 2 * HEAD_DIM]
    v_pos = pos_rows[:, 2 * HEAD_DIM :]
    doc_start = document_starts(doc_lengths, tokens)
    context = attend(q_pos, k_pos, v_pos, doc_start, doc_most)
    slotted = context.at[order].get(mode="promise_in_bounds", unique_indices=True)
    returned = lax.all_to_all(slotted, ("z", "y"), split_axis=0, concat_axis=1, tiled=True)
    return returned.reshape(tok_rows, HEADS * HEAD_DIM)


def solution(mesh):
    dp_size, ctx_size = mesh.devices.shape
    grid = Mesh(mesh.devices.reshape(dp_size, KV_HEADS, ctx_size // KV_HEADS), ("dp", "z", "y"))
    rows = P(("dp", "z", "y"), None)
    placed = (rows, rows, rows, P("dp"), P("dp"))
    return jax.shard_map(per_device, mesh=grid, in_specs=placed, out_specs=rows, check_vma=False)
```

profile of v0, /device:TPU:6, one launch (start us, length us, event | category | flops | bytes accessed | tf_op | source)
XLA Modules:
  0.0 322.4 jit_solution(10956242489249688163)
XLA Ops:
  6.5 0.0 all-gather.2.cloned.1.call-start
  6.5 1.1 copy.41
  7.7 1.1 copy.42
  8.8 0.1 pad_maximum_fusion.1
  8.8 0.3 copy.43
  9.1 0.0 copy-start.1
  9.1 27.7 %all_to_all.52 = bf16[128,8,2,128]{3,0,2,1:T(8,128)(2,1)S(1)} all-to-all(bf16[128,8,2,128]{3,0,2,1:T(8,128)(2,1)S(1)} %copy.43), channel_id=1, replica_groups=mesh['dp'=8,'z'=8,'y'=8] {'z'}, dimensions={1} | all-to-all | bytes 1048576 | tf_op jit(solution)/shard_map/all_to_all | solution.py:74
  36.9 1.3 copy.45
  38.3 0.0 all-gather.2.cloned.1.call-update
  38.3 0.0 copy-done.1
  38.3 2.4 copy.38
  40.7 0.0 copy-start.3
  40.7 8.4 %all-to-all-start = ((bf16[128,64,128]{0,2,1:T(8,128)(2,1)}), bf16[128,64,128]{0,2,1:T(8,128)(2,1)S(1)}, u32[]{:S(2)}, u32[]{:S(2)}) async-start(bf16[128,64,128]{0,2,1:T(8,128)(2,1)} %bitcast.33), calls=%async_computation | async-start | bytes 4194304 | tf_op jit(solution)/shard_map/all_to_all | solution.py:67
  49.2 0.0 copy-done.3
  49.2 0.1 copy.46
  49.3 0.1 reduce
  49.4 0.2 convert_reduce_fusion
  49.6 0.2 select_reduce_fusion
  49.8 0.0 copy-start.2
  49.8 2.7 copy.47.ds_ref
  52.5 0.0 copy-done.2
  52.5 6.8 %sort.15 = (s32[8192]{0:T(1024)}, s32[8192]{0:T(1024)S(1)}) sort(s32[8192]{0:T(1024)S(1)} %copy-done.2, s32[8192]{0:T(1024)S(1)} %iota.11), dimensions={0}, to_apply=%region_0.0 | sort | flops 106496 | bytes 131072 | tf_op jit(solution)/shard_map/sort | solution.py:79
  59.2 0.1 fusion.4
  59.3 61.8 %all-to-all-done = bf16[128,64,128]{0,2,1:T(8,128)(2,1)S(1)} async-done(((bf16[128,64,128]{0,2,1:T(8,128)(2,1)}), bf16[128,64,128]{0,2,1:T(8,128)(2,1)S(1)}, u32[]{:S(2)}, u32[]{:S(2)}) %all-to-all-start) | async-done | bytes 2097184 | tf_op jit(solution)/shard_map/all_to_all | solution.py:67
  121.1 2.6 copy.40
  123.7 12.2 %all-gather.2.cloned.1.call-done = bf16[8192,1,2,128]{3,2,1,0:T(2,128)(2,1)} async-done(((bf16[1024,1,2,128]{3,2,1,0:T(2,128)(2,1)}), bf16[8192,1,2,128]{3,2,1,0:T(2,128)(2,1)}) %all-gather.2.cloned.1.call-update) | async-done | bytes 4194320 | tf_op jit(solution)/shard_map/all_gather | solution.py:75
  136.0 0.0 copy-start
  136.0 2.9 copy.54
  138.8 0.0 copy-done
  138.9 3.5 %pad_maximum_fusion = bf16[8192,384]{1,0:T(8,128)(2,1)} fusion(bf16[8192,256]{1,0:T(8,128)(2,1)S(1)} %bitcast.30, bf16[8192,128]{1,0:T(8,128)(2,1)S(1)} %bitcast.34), kind=kLoop, calls=%fused_computation.2 | loop fusion | flops 12582912 | bytes 12582912 | tf_op jit(solution)/shard_map/concatenate | solution.py:76
  142.3 36.0 %gather_fusion = bf16[8192,384]{1,0:T(8,128)(2,1)} fusion(bf16[8192,384]{1,0:T(8,128)(2,1)} %pad_maximum_fusion, s32[8192]{0:T(1024)S(1)} %fusion.4), kind=kCustom, calls=%fused_computation | custom fusion | bytes 12615680 | tf_op jit(solution)/shard_map/gather | solution.py:82
  178.3 5.8 %fusion.12 = (bf16[8192,128]{1,0:T(8,128)(2,1)}, bf16[8192,128]{1,0:T(8,128)(2,1)}, bf16[8192,128]{1,0:T(8,128)(2,1)}) fusion(bf16[8192,384]{1,0:T(8,128)(2,1)} %gather_fusion), kind=kLoop, calls=%fused_computation.36 | loop fusion | bytes 12582912 | tf_op jit(solution)/shard_map/slice | solution.py:85
  184.1 43.6 %shard_map.55 = bf16[8192,128]{1,0:T(8,128)(2,1)} custom-call(bf16[8192,128]{1,0:T(8,128)(2,1)} %get-tuple-element.9.q_ref, bf16[8192,128]{1,0:T(8,128)(2,1)} %get-tuple-element.8.k_ref, bf16[8192,128]{1,0:T(8,128)(2,1)} %get-tuple-element.7.v_ref, s32[8192,1]{1,0:T(8,128)} %copy.47.ds_ref), custom_call_target="tpu_custom_call" | custom-call | tf_op jit(solution)/shard_map/pallas_call | solution.py:47
  227.7 23.8 %gather_fusion.1 = bf16[8192,128]{1,0:T(8,128)(2,1)S(1)} fusion(bf16[8192,128]{1,0:T(8,128)(2,1)} %shard_map.55, s32[8192]{0:T(1024)S(1)} %fusion.5), kind=kCustom, calls=%fused_computation.1 | custom fusion | bytes 4227072 | tf_op jit(solution)/shard_map/gather | solution.py:88
  251.5 62.5 %all_to_all.53 = bf16[64,128,128]{2,1,0:T(8,128)(2,1)S(1)} all-to-all(bf16[64,128,128]{2,1,0:T(8,128)(2,1)S(1)} %bitcast.31), channel_id=1, replica_groups=mesh['dp'=8,'z'=8,'y'=8] {'z','y'}, dimensions={0} | all-to-all | bytes 4194304 | tf_op jit(solution)/shard_map/all_to_all | solution.py:89
  314.0 1.6 copy_bitcast_fusion.1
  (5 shorter events, 0.1 us)
Async XLA Ops:
  6.5 129.4 %all-gather.2.cloned.1.call-start = ((), (), s32[]{:S(2)}) async-start(), calls=%async_computation.3 | async-start | bytes 4718592 | tf_op jit(solution)/shard_map/all_gather | solution.py:75
  9.1 29.2 %copy-start.1 = (bf16[128,8192]{1,0:T(8,128)(2,1)S(1)}, bf16[128,8192]{1,0:T(8,128)(2,1)}, u32[]{:S(2)}) copy-start(bf16[128,8192]{1,0:T(8,128)(2,1)} %param.5) | copy-start | bytes 6291460
  40.7 8.4 %copy-start.3 = (s32[16]{0:T(128)S(1)}, s32[16]{0:T(128)}, u32[]{:S(2)}) copy-start(s32[16]{0:T(128)} %param.9) | copy-start | bytes 196
  40.7 80.4 %all-to-all-start = ((bf16[128,64,128]{0,2,1:T(8,128)(2,1)}), bf16[128,64,128]{0,2,1:T(8,128)(2,1)S(1)}, u32[]{:S(2)}, u32[]{:S(2)}) async-start(bf16[128,64,128]{0,2,1:T(8,128)(2,1)} %bitcast.33), calls=%async_computation | async-start | bytes 4194304 | tf_op jit(solution)/shard_map/all_to_all | solution.py:67
  49.8 2.7 copy-start.2
  136.0 2.9 copy-start
Sparse Core Ops, SparseCore 0:
  38.4 97.5 all-gather.1
where the time goes:
time: 324 us; the launch traced here: 322 us
  blocking collectives  90.3 us (28%)
  local copies, waits for them, and re-layouts  81.7 us (25%)
  waiting for transfers between devices  74.1 us (23%)
  Pallas kernels  43.6 us (13%)
  between operations  13.5 us (4%)
  other arithmetic  10.9 us (3%)
  starting transfers between devices  8.42 us (3%)
    all_to_all x1, blocking collectives, per_device(): lax.all_to_all(slotted, ('z', 'y'), split_axis=0, concat_axis=1, tiled=True)  62.5 us
    all_to_all x1, waiting for transfers between devices, per_device(): lax.all_to_all(query_split, ('z', 'y'), split_axis=1, concat_axis=0, tile...  61.8 us
    pallas_call x1, Pallas kernels, attend(): pl.pallas_call(functools.partial(attn_kernel, doc_most), grid=(tokens //...  43.6 us
    gather x1, local copies, waits for them, and re-layouts, per_device(): joined.at[ring_row].get(mode='promise_in_bounds', unique_indices=True)  36 us
    all_to_all x1, blocking collectives, per_device(): lax.all_to_all(paired, 'z', split_axis=1, concat_axis=0, tiled=True)  27.7 us
    gather x1, local copies, waits for them, and re-layouts, per_device(): context.at[order].get(mode='promise_in_bounds', unique_indices=True)  23.8 us
    all_gather x1, waiting for transfers between devices, per_device(): lax.all_gather(kv_col, 'y', axis=0, tiled=True)  12.2 us
    all_to_all x1, starting transfers between devices, per_device(): lax.all_to_all(query_split, ('z', 'y'), split_axis=1, concat_axis=0, tile...  8.42 us
  transfers between devices with their start and end apart: 2, of which 2 were waited for; matrix products, arithmetic and copies ran while one was open for 5% of the time, Pallas kernels for 0%

commit v1 on v0

--- a/solution.py
+++ b/solution.py
@@ -4,6 +4,7 @@
 import jax.numpy as jnp
 from jax import lax
 from jax.experimental import pallas as pl
+from jax.experimental.pallas import tpu as pltpu
 from jax.sharding import Mesh
 from jax.sharding import PartitionSpec as P
 
@@ -23,39 +24,77 @@
     return jnp.sum(jnp.where(matches, doc_firsts[None, :], 0), axis=1)
 
 
-def attn_kernel(doc_most, q_ref, k_ref, v_ref, ds_ref, o_ref):
+def attn_kernel(doc_most, first_ref, q_ref, k_ref, v_ref, ds_ref, o_ref, s_scr, m_scr, l_scr, acc_scr):
     b = pl.program_id(0)
-    window = doc_most + BLOCK
+    tiles = doc_most // BLOCK + 1
     start = pl.multiple_of(jnp.maximum(b * BLOCK - doc_most, 0), BLOCK)
+    q_first = b * BLOCK
+    ds_first = first_ref[b]
     q = q_ref[...]
-    k = k_ref[pl.ds(start, window), :]
-    v = v_ref[pl.ds(start, window), :]
-    s = lax.dot_general(q, k, (((1,), (1,)), ((), ())), preferred_element_type=jnp.float32)
-    s = s * (HEAD_DIM ** (-0.5))
-    qpos = b * BLOCK + lax.broadcasted_iota(jnp.int32, (BLOCK, window), 0)
-    kpos = start + lax.broadcasted_iota(jnp.int32, (BLOCK, window), 1)
-    visible = (kpos <= qpos) & (kpos >= ds_ref[...])
-    s = jnp.where(visible, s, -jnp.inf)
-    m = jnp.max(s, axis=1, keepdims=True)
-    e = jnp.exp(s - m)
-    l = jnp.sum(e, axis=1, keepdims=True)
-    w = (e / l).astype(jnp.bfloat16)
-    o_ref[...] = jnp.dot(w, v, preferred_element_type=jnp.float32).astype(o_ref.dtype)
+    qpos = q_first + lax.broadcasted_iota(jnp.int32, (BLOCK, BLOCK), 0)
+    ds = ds_ref[...]
+    m_scr[...] = jnp.full(m_scr.shape, -jnp.inf, jnp.float32)
+    l_scr[...] = jnp.zeros(l_scr.shape, jnp.float32)
+    acc_scr[...] = jnp.zeros(acc_scr.shape, jnp.float32)
+    needed = []
+    for t in range(tiles):
+        key_first = start + t * BLOCK
+        needed.append((key_first + BLOCK - 1 >= ds_first) & (key_first <= q_first + BLOCK - 1))
+    for t in range(tiles):
+        key_first = start + t * BLOCK
 
-def attend(q, k, v, doc_start, doc_most):
-    tokens = q.shape[0]
+        @pl.when(needed[t])
+        def _():
+            k = k_ref[pl.ds(pl.multiple_of(key_first, BLOCK), BLOCK), :]
+            s = lax.dot_general(q, k, (((1,), (1,)), ((), ())), preferred_element_type=jnp.float32)
+            s = s * (HEAD_DIM ** (-0.5))
+            kpos = key_first + lax.broadcasted_iota(jnp.int32, (BLOCK, BLOCK), 1)
+            s = jnp.where((kpos <= qpos) & (kpos >= ds), s, -jnp.inf)
+            s_scr[t] = s
+            m_scr[...] = jnp.maximum(m_scr[...], jnp.max(s, axis=1, keepdims=True))
+    for t in range(tiles):
+        @pl.when(needed[t])
+        def _():
+            e = jnp.exp(s_scr[t] - m_scr[...])
+            s_scr[t] = e
+            l_scr[...] += jnp.sum(e, axis=1, keepdims=True)
+    for t in range(tiles):
+        key_first = start + t * BLOCK
+
+        @pl.when(needed[t])
+        def _():
+            v = v_ref[pl.ds(pl.multiple_of(key_first, BLOCK), BLOCK), :]
+            w = (s_scr[t] / l_scr[...]).astype(jnp.bfloat16)
+            acc_scr[...] += jnp.dot(w, v, preferred_element_type=jnp.float32)
+    o_ref[...] = acc_scr[...].astype(o_ref.dtype)
+
+
+def attend(rows, doc_start, doc_most):
+    tokens = rows.shape[0]
+    tiles = doc_most // BLOCK + 1
+    grid_spec = pltpu.PrefetchScalarGridSpec(
+        num_scalar_prefetch=1,
+        grid=(tokens // BLOCK,),
+        in_specs=[
+            pl.BlockSpec((BLOCK, HEAD_DIM), lambda b, f: (b, 0)),
+            pl.BlockSpec((tokens, HEAD_DIM), lambda b, f: (0, 1)),
+            pl.BlockSpec((tokens, HEAD_DIM), lambda b, f: (0, 2)),
+            pl.BlockSpec((BLOCK, 1), lambda b, f: (b, 0)),
+        ],
+        out_specs=pl.BlockSpec((BLOCK, HEAD_DIM), lambda b, f: (b, 0)),
+        scratch_shapes=[
+            pltpu.VMEM((tiles, BLOCK, BLOCK), jnp.float32),
+            pltpu.VMEM((BLOCK, 1), jnp.float32),
+            pltpu.VMEM((BLOCK, 1), jnp.float32),
+            pltpu.VMEM((BLOCK, HEAD_DIM), jnp.float32),
+        ],
+    )
+    block_firsts = doc_start.reshape(tokens // BLOCK, BLOCK)[:, 0]
     return pl.pallas_call(
         functools.partial(attn_kernel, doc_most),
-        grid=(tokens // BLOCK,),
-        in_specs=[
-            pl.BlockSpec((BLOCK, HEAD_DIM), lambda b: (b, 0)),
-            pl.BlockSpec((tokens, HEAD_DIM), lambda b: (0, 0)),
-            pl.BlockSpec((tokens, HEAD_DIM), lambda b: (0, 0)),
-            pl.BlockSpec((BLOCK, 1), lambda b: (b, 0)),
-        ],
-        out_specs=pl.BlockSpec((BLOCK, HEAD_DIM), lambda b: (b, 0)),
+        grid_spec=grid_spec,
         out_shape=jax.ShapeDtypeStruct((tokens, HEAD_DIM), jnp.bfloat16),
-    )(q, k, v, doc_start.reshape(tokens, 1))
+    )(block_firsts, rows, rows, rows, doc_start.reshape(tokens, 1))
 
 
 def per_device(queries, keys, values, order, doc_lengths):
@@ -80,11 +119,8 @@
     slot_dev = slot_of // tok_rows
     ring_row = (slot_dev % ny) * (nz * tok_rows) + (slot_dev // ny) * tok_rows + slot_of % tok_rows
     pos_rows = joined.at[ring_row].get(mode="promise_in_bounds", unique_indices=True)
-    q_pos = pos_rows[:, :HEAD_DIM]
-    k_pos = pos_rows[:, HEAD_DIM : 2 * HEAD_DIM]
-    v_pos = pos_rows[:, 2 * HEAD_DIM :]
     doc_start = document_starts(doc_lengths, tokens)
-    context = attend(q_pos, k_pos, v_pos, doc_start, doc_most)
+    context = attend(pos_rows, doc_start, doc_most)
     slotted = context.at[order].get(mode="promise_in_bounds", unique_indices=True)
     returned = lax.all_to_all(slotted, ("z", "y"), split_axis=0, concat_axis=1, tiled=True)
     return returned.reshape(tok_rows, HEADS * HEAD_DIM)

time: 324 us -> 322 us (level)
  local copies, waits for them, and re-layouts: 81.7 us -> 76.6 us
    slice x1, local copies, waits for them, and re-layouts: 5.77 us -> 0.62 us  [attend(): block_firsts = doc_start.reshape(tokens // BLOCK, BLOCK)[:, 0]]
where the time goes in v1:
time: 322 us; the launch traced here: 317 us
  blocking collectives  90.7 us (28%)
  local copies, waits for them, and re-layouts  76.6 us (24%)
  waiting for transfers between devices  73.4 us (23%)
  Pallas kernels  43.8 us (14%)
  between operations  13.5 us (4%)
  other arithmetic  10.9 us (3%)
  starting transfers between devices  8.42 us (3%)
    all_to_all x1, blocking collectives, per_device(): lax.all_to_all(slotted, ('z', 'y'), split_axis=0, concat_axis=1, tiled=True)  63 us
    all_to_all x1, waiting for transfers between devices, per_device(): lax.all_to_all(query_split, ('z', 'y'), split_axis=1, concat_axis=0, tile...  61.2 us
    pallas_call x1, Pallas kernels, attend(): pl.pallas_call(functools.partial(attn_kernel, doc_most), grid_spec=grid_s...  43.8 us
    gather x1, local copies, waits for them, and re-layouts, per_device(): joined.at[ring_row].get(mode='promise_in_bounds', unique_indices=True)  36 us
    all_to_all x1, blocking collectives, per_device(): lax.all_to_all(paired, 'z', split_axis=1, concat_axis=0, tiled=True)  27.7 us
    gather x1, local copies, waits for them, and re-layouts, per_device(): context.at[order].get(mode='promise_in_bounds', unique_indices=True)  23.8 us
    all_gather x1, waiting for transfers between devices, per_device(): lax.all_gather(kv_col, 'y', axis=0, tiled=True)  12.3 us
    all_to_all x1, starting transfers between devices, per_device(): lax.all_to_all(query_split, ('z', 'y'), split_axis=1, concat_axis=0, tile...  8.42 us
  transfers between devices with their start and end apart: 2, of which 2 were waited for; matrix products, arithmetic and copies ran while one was open for 5% of the time, Pallas kernels for 0%

profile of v1, /device:TPU:6, one launch (start us, length us, event | category | flops | bytes accessed | tf_op | source)
XLA Modules:
  0.0 317.4 jit_solution(8301281144369007332)
XLA Ops:
  6.5 0.0 all-gather.2.cloned.1.call-start
  6.5 1.1 copy.43
  7.7 1.1 copy.42
  8.8 0.1 pad_maximum_fusion.1
  8.8 0.3 copy.44
  9.1 0.0 copy-start.1
  9.1 27.7 %all_to_all.52 = bf16[128,8,2,128]{3,0,2,1:T(8,128)(2,1)S(1)} all-to-all(bf16[128,8,2,128]{3,0,2,1:T(8,128)(2,1)S(1)} %copy.44), channel_id=1, replica_groups=mesh['dp'=8,'z'=8,'y'=8] {'z'}, dimensions={1} | all-to-all | bytes 1048576 | tf_op jit(solution)/shard_map/all_to_all | solution.py:113
  36.9 1.3 copy.46
  38.3 0.0 all-gather.2.cloned.1.call-update
  38.3 0.0 copy-done.1
  38.3 2.4 copy.39
  40.7 0.0 copy-start.3
  40.7 8.4 %all-to-all-start = ((bf16[128,64,128]{0,2,1:T(8,128)(2,1)}), bf16[128,64,128]{0,2,1:T(8,128)(2,1)S(1)}, u32[]{:S(2)}, u32[]{:S(2)}) async-start(bf16[128,64,128]{0,2,1:T(8,128)(2,1)} %bitcast.33), calls=%async_computation | async-start | bytes 4194304 | tf_op jit(solution)/shard_map/all_to_all | solution.py:106
  49.2 0.0 copy-done.3
  49.2 0.1 copy.38
  49.3 0.1 reduce
  49.4 0.2 convert_reduce_fusion
  49.6 0.2 select_reduce_fusion
  49.8 0.0 copy-start.2
  49.8 2.7 copy.47.ds_ref
  52.5 0.0 copy-done.2
  52.5 6.8 %sort.15 = (s32[8192]{0:T(1024)}, s32[8192]{0:T(1024)S(1)}) sort(s32[8192]{0:T(1024)S(1)} %copy-done.2, s32[8192]{0:T(1024)S(1)} %iota.11), dimensions={0}, to_apply=%region_3.4 | sort | flops 106496 | bytes 131072 | tf_op jit(solution)/shard_map/sort | solution.py:118
  59.2 0.6 slice_reduce_fusion.first_ref
  59.9 0.1 fusion.4
  60.0 61.2 %all-to-all-done = bf16[128,64,128]{0,2,1:T(8,128)(2,1)S(1)} async-done(((bf16[128,64,128]{0,2,1:T(8,128)(2,1)}), bf16[128,64,128]{0,2,1:T(8,128)(2,1)S(1)}, u32[]{:S(2)}, u32[]{:S(2)}) %all-to-all-start) | async-done | bytes 2097184 | tf_op jit(solution)/shard_map/all_to_all | solution.py:106
  121.1 2.6 copy.41
  123.7 12.3 %all-gather.2.cloned.1.call-done = bf16[8192,1,2,128]{3,2,1,0:T(2,128)(2,1)} async-done(((bf16[1024,1,2,128]{3,2,1,0:T(2,128)(2,1)}), bf16[8192,1,2,128]{3,2,1,0:T(2,128)(2,1)}) %all-gather.2.cloned.1.call-update) | async-done | bytes 4194320 | tf_op jit(solution)/shard_map/all_gather | solution.py:114
  136.0 0.0 copy-start
  136.0 2.9 copy.54
  138.8 0.0 copy-done
  138.9 3.5 %pad_maximum_fusion = bf16[8192,384]{1,0:T(8,128)(2,1)} fusion(bf16[8192,256]{1,0:T(8,128)(2,1)S(1)} %bitcast.30, bf16[8192,128]{1,0:T(8,128)(2,1)S(1)} %bitcast.34), kind=kLoop, calls=%fused_computation.2 | loop fusion | flops 12582912 | bytes 12582912 | tf_op jit(solution)/shard_map/concatenate | solution.py:115
  142.3 36.0 %gather_fusion = bf16[8192,384]{1,0:T(8,128)(2,1)} fusion(bf16[8192,384]{1,0:T(8,128)(2,1)} %pad_maximum_fusion, s32[8192]{0:T(1024)S(1)} %fusion.4), kind=kCustom, calls=%fused_computation | custom fusion | bytes 12615680 | tf_op jit(solution)/shard_map/gather | solution.py:121
  178.3 43.8 %shard_map.55 = bf16[8192,128]{1,0:T(8,128)(2,1)} custom-call(s32[16]{0:T(128)} %slice_reduce_fusion.first_ref, bf16[8192,384]{1,0:T(8,128)(2,1)} %gather_fusion, bf16[8192,384]{1,0:T(8,128)(2,1)} %gather_fusion, bf16[8192,384]{1,0:T(8,128)(2,1)} %gather_fusion, s32[8192,1]{1,0:T(8,128)} %copy.47.ds_ref), custom_call_target="tpu_custom_call" | custom-call | tf_op jit(solution)/shard_map/pallas_call | solution.py:93
  222.2 23.8 %gather_fusion.1 = bf16[8192,128]{1,0:T(8,128)(2,1)S(1)} fusion(bf16[8192,128]{1,0:T(8,128)(2,1)} %shard_map.55, s32[8192]{0:T(1024)S(1)} %fusion.5), kind=kCustom, calls=%fused_computation.1 | custom fusion | bytes 4227072 | tf_op jit(solution)/shard_map/gather | solution.py:124
  245.9 63.0 %all_to_all.53 = bf16[64,128,128]{2,1,0:T(8,128)(2,1)S(1)} all-to-all(bf16[64,128,128]{2,1,0:T(8,128)(2,1)S(1)} %bitcast.31), channel_id=1, replica_groups=mesh['dp'=8,'z'=8,'y'=8] {'z','y'}, dimensions={0} | all-to-all | bytes 4194304 | tf_op jit(solution)/shard_map/all_to_all | solution.py:125
  308.9 1.6 copy_bitcast_fusion.1
  (6 shorter events, 0.1 us)
Async XLA Ops:
  6.5 129.4 %all-gather.2.cloned.1.call-start = ((), (), s32[]{:S(2)}) async-start(), calls=%async_computation.3 | async-start | bytes 4718592 | tf_op jit(solution)/shard_map/all_gather | solution.py:114
  9.1 29.2 %copy-start.1 = (bf16[128,8192]{1,0:T(8,128)(2,1)S(1)}, bf16[128,8192]{1,0:T(8,128)(2,1)}, u32[]{:S(2)}) copy-start(bf16[128,8192]{1,0:T(8,128)(2,1)} %param.5) | copy-start | bytes 6291460
  40.7 8.4 %copy-start.3 = (s32[16]{0:T(128)S(1)}, s32[16]{0:T(128)}, u32[]{:S(2)}) copy-start(s32[16]{0:T(128)} %param.9) | copy-start | bytes 196
  40.7 80.4 %all-to-all-start = ((bf16[128,64,128]{0,2,1:T(8,128)(2,1)}), bf16[128,64,128]{0,2,1:T(8,128)(2,1)S(1)}, u32[]{:S(2)}, u32[]{:S(2)}) async-start(bf16[128,64,128]{0,2,1:T(8,128)(2,1)} %bitcast.33), calls=%async_computation | async-start | bytes 4194304 | tf_op jit(solution)/shard_map/all_to_all | solution.py:106
  49.8 2.7 copy-start.2
  136.0 2.9 copy-start
Sparse Core Ops, SparseCore 0:
  38.4 97.5 all-gather.1

commit v2 on v1

--- a/solution.py
+++ b/solution.py
@@ -58,13 +58,14 @@
             e = jnp.exp(s_scr[t] - m_scr[...])
             s_scr[t] = e
             l_scr[...] += jnp.sum(e, axis=1, keepdims=True)
+    l_scr[...] = 1.0 / l_scr[...]
     for t in range(tiles):
         key_first = start + t * BLOCK
 
         @pl.when(needed[t])
         def _():
             v = v_ref[pl.ds(pl.multiple_of(key_first, BLOCK), BLOCK), :]
-            w = (s_scr[t] / l_scr[...]).astype(jnp.bfloat16)
+            w = (s_scr[t] * l_scr[...]).astype(jnp.bfloat16)
             acc_scr[...] += jnp.dot(w, v, preferred_element_type=jnp.float32)
     o_ref[...] = acc_scr[...].astype(o_ref.dtype)
 

time: 322 us -> 322 us (level)
  the two profiles are of different devices: /device:TPU:6 before, /device:TPU:43 now
where the time goes in v2:
time: 322 us
  blocking collectives  94.7 us (29%)
  local copies, waits for them, and re-layouts  76.6 us (24%)
  waiting for transfers between devices  73.6 us (23%)
  Pallas kernels  44.2 us (14%)
  between operations  13.5 us (4%)
  other arithmetic  10.9 us (3%)
  starting transfers between devices  8.25 us (3%)
    all_to_all x1, blocking collectives, per_device(): lax.all_to_all(slotted, ('z', 'y'), split_axis=0, concat_axis=1, tiled=True)  68.7 us
    all_to_all x1, waiting for transfers between devices, per_device(): lax.all_to_all(query_split, ('z', 'y'), split_axis=1, concat_axis=0, tile...  58.4 us
    pallas_call x1, Pallas kernels, attend(): pl.pallas_call(functools.partial(attn_kernel, doc_most), grid_spec=grid_s...  44.2 us
    gather x1, local copies, waits for them, and re-layouts, per_device(): joined.at[ring_row].get(mode='promise_in_bounds', unique_indices=True)  36 us
    all_to_all x1, blocking collectives, per_device(): lax.all_to_all(paired, 'z', split_axis=1, concat_axis=0, tiled=True)  26.1 us
    gather x1, local copies, waits for them, and re-layouts, per_device(): context.at[order].get(mode='promise_in_bounds', unique_indices=True)  23.8 us
    all_gather x1, waiting for transfers between devices, per_device(): lax.all_gather(kv_col, 'y', axis=0, tiled=True)  15.1 us
    all_to_all x1, starting transfers between devices, per_device(): lax.all_to_all(query_split, ('z', 'y'), split_axis=1, concat_axis=0, tile...  8.25 us
  transfers between devices with their start and end apart: 2, of which 2 were waited for; matrix products, arithmetic and copies ran while one was open for 5% of the time, Pallas kernels for 0%

profile of v2, /device:TPU:43, one launch (start us, length us, event | category | flops | bytes accessed | tf_op | source)
XLA Modules:
  0.0 321.8 jit_solution(12256320088809297065)
XLA Ops:
  6.5 0.0 all-gather.2.cloned.1.call-start
  6.5 1.1 copy.43
  7.7 1.1 copy.42
  8.8 0.1 pad_maximum_fusion.1
  8.8 0.3 copy.44
  9.1 0.0 copy-start.1
  9.1 26.1 %all_to_all.52 = bf16[128,8,2,128]{3,0,2,1:T(8,128)(2,1)S(1)} all-to-all(bf16[128,8,2,128]{3,0,2,1:T(8,128)(2,1)S(1)} %copy.44), channel_id=1, replica_groups=mesh['dp'=8,'z'=8,'y'=8] {'z'}, dimensions={1} | all-to-all | bytes 1048576 | tf_op jit(solution)/shard_map/all_to_all | solution.py:114
  35.3 1.3 copy.46
  36.6 0.0 all-gather.2.cloned.1.call-update
  36.6 0.0 copy-done.1
  36.6 2.4 copy.39
  39.1 0.0 copy-start.3
  39.1 8.3 %all-to-all-start = ((bf16[128,64,128]{0,2,1:T(8,128)(2,1)}), bf16[128,64,128]{0,2,1:T(8,128)(2,1)S(1)}, u32[]{:S(2)}, u32[]{:S(2)}) async-start(bf16[128,64,128]{0,2,1:T(8,128)(2,1)} %bitcast.33), calls=%async_computation | async-start | bytes 4194304 | tf_op jit(solution)/shard_map/all_to_all | solution.py:107
  47.3 0.0 copy-done.3
  47.3 0.1 copy.38
  47.5 0.1 reduce
  47.6 0.2 convert_reduce_fusion
  47.8 0.2 select_reduce_fusion
  48.0 0.0 copy-start.2
  48.0 2.7 copy.47.ds_ref
  50.6 0.0 copy-done.2
  50.6 6.8 %sort.15 = (s32[8192]{0:T(1024)}, s32[8192]{0:T(1024)S(1)}) sort(s32[8192]{0:T(1024)S(1)} %copy-done.2, s32[8192]{0:T(1024)S(1)} %iota.11), dimensions={0}, to_apply=%region_3.4 | sort | flops 106496 | bytes 131072 | tf_op jit(solution)/shard_map/sort | solution.py:119
  57.4 0.6 slice_reduce_fusion.first_ref
  58.0 0.1 fusion.4
  58.1 58.4 %all-to-all-done = bf16[128,64,128]{0,2,1:T(8,128)(2,1)S(1)} async-done(((bf16[128,64,128]{0,2,1:T(8,128)(2,1)}), bf16[128,64,128]{0,2,1:T(8,128)(2,1)S(1)}, u32[]{:S(2)}, u32[]{:S(2)}) %all-to-all-start) | async-done | bytes 2097184 | tf_op jit(solution)/shard_map/all_to_all | solution.py:107
  116.5 2.6 copy.41
  119.1 15.1 %all-gather.2.cloned.1.call-done = bf16[8192,1,2,128]{3,2,1,0:T(2,128)(2,1)} async-done(((bf16[1024,1,2,128]{3,2,1,0:T(2,128)(2,1)}), bf16[8192,1,2,128]{3,2,1,0:T(2,128)(2,1)}) %all-gather.2.cloned.1.call-update) | async-done | bytes 4194320 | tf_op jit(solution)/shard_map/all_gather | solution.py:115
  134.3 0.0 copy-start
  134.3 2.9 copy.54
  137.2 0.0 copy-done
  137.2 3.5 %pad_maximum_fusion = bf16[8192,384]{1,0:T(8,128)(2,1)} fusion(bf16[8192,256]{1,0:T(8,128)(2,1)S(1)} %bitcast.30, bf16[8192,128]{1,0:T(8,128)(2,1)S(1)} %bitcast.34), kind=kLoop, calls=%fused_computation.2 | loop fusion | flops 12582912 | bytes 12582912 | tf_op jit(solution)/shard_map/concatenate | solution.py:116
  140.6 36.0 %gather_fusion = bf16[8192,384]{1,0:T(8,128)(2,1)} fusion(bf16[8192,384]{1,0:T(8,128)(2,1)} %pad_maximum_fusion, s32[8192]{0:T(1024)S(1)} %fusion.4), kind=kCustom, calls=%fused_computation | custom fusion | bytes 12615680 | tf_op jit(solution)/shard_map/gather | solution.py:122
  176.7 44.2 %shard_map.55 = bf16[8192,128]{1,0:T(8,128)(2,1)} custom-call(s32[16]{0:T(128)} %slice_reduce_fusion.first_ref, bf16[8192,384]{1,0:T(8,128)(2,1)} %gather_fusion, bf16[8192,384]{1,0:T(8,128)(2,1)} %gather_fusion, bf16[8192,384]{1,0:T(8,128)(2,1)} %gather_fusion, s32[8192,1]{1,0:T(8,128)} %copy.47.ds_ref), custom_call_target="tpu_custom_call" | custom-call | tf_op jit(solution)/shard_map/pallas_call | solution.py:94
  220.9 23.8 %gather_fusion.1 = bf16[8192,128]{1,0:T(8,128)(2,1)S(1)} fusion(bf16[8192,128]{1,0:T(8,128)(2,1)} %shard_map.55, s32[8192]{0:T(1024)S(1)} %fusion.5), kind=kCustom, calls=%fused_computation.1 | custom fusion | bytes 4227072 | tf_op jit(solution)/shard_map/gather | solution.py:125
  244.7 68.7 %all_to_all.53 = bf16[64,128,128]{2,1,0:T(8,128)(2,1)S(1)} all-to-all(bf16[64,128,128]{2,1,0:T(8,128)(2,1)S(1)} %bitcast.31), channel_id=1, replica_groups=mesh['dp'=8,'z'=8,'y'=8] {'z','y'}, dimensions={0} | all-to-all | bytes 4194304 | tf_op jit(solution)/shard_map/all_to_all | solution.py:126
  313.3 1.6 copy_bitcast_fusion.1
  (6 shorter events, 0.1 us)
Async XLA Ops:
  6.5 127.7 %all-gather.2.cloned.1.call-start = ((), (), s32[]{:S(2)}) async-start(), calls=%async_computation.3 | async-start | bytes 4718592 | tf_op jit(solution)/shard_map/all_gather | solution.py:115
  9.1 27.5 %copy-start.1 = (bf16[128,8192]{1,0:T(8,128)(2,1)S(1)}, bf16[128,8192]{1,0:T(8,128)(2,1)}, u32[]{:S(2)}) copy-start(bf16[128,8192]{1,0:T(8,128)(2,1)} %param.5) | copy-start | bytes 6291460
  39.1 8.3 %copy-start.3 = (s32[16]{0:T(128)S(1)}, s32[16]{0:T(128)}, u32[]{:S(2)}) copy-start(s32[16]{0:T(128)} %param.9) | copy-start | bytes 196
  39.1 77.5 %all-to-all-start = ((bf16[128,64,128]{0,2,1:T(8,128)(2,1)}), bf16[128,64,128]{0,2,1:T(8,128)(2,1)S(1)}, u32[]{:S(2)}, u32[]{:S(2)}) async-start(bf16[128,64,128]{0,2,1:T(8,128)(2,1)} %bitcast.33), calls=%async_computation | async-start | bytes 4194304 | tf_op jit(solution)/shard_map/all_to_all | solution.py:107
  48.0 2.7 copy-start.2
  134.3 2.9 copy-start
Sparse Core Ops, SparseCore 0:
  36.7 97.4 all-gather.1

commit v3 on v2

--- a/solution.py
+++ b/solution.py
@@ -24,9 +24,13 @@
     return jnp.sum(jnp.where(matches, doc_firsts[None, :], 0), axis=1)
 
 
-def attn_kernel(doc_most, first_ref, q_ref, k_ref, v_ref, ds_ref, o_ref, s_scr, m_scr, l_scr, acc_scr):
+def attn_kernel(doc_most, first_ref, *refs):
+    tiles = doc_most // BLOCK + 1
+    q_ref = refs[0]
+    k_refs = refs[1 : 1 + tiles]
+    v_refs = refs[1 + tiles : 1 + 2 * tiles]
+    ds_ref, o_ref, s_scr, m_scr, l_scr, acc_scr = refs[1 + 2 * tiles :]
     b = pl.program_id(0)
-    tiles = doc_most // BLOCK + 1
     start = pl.multiple_of(jnp.maximum(b * BLOCK - doc_most, 0), BLOCK)
     q_first = b * BLOCK
     ds_first = first_ref[b]
@@ -45,7 +49,7 @@
 
         @pl.when(needed[t])
         def _():
-            k = k_ref[pl.ds(pl.multiple_of(key_first, BLOCK), BLOCK), :]
+            k = k_refs[t][...]
             s = lax.dot_general(q, k, (((1,), (1,)), ((), ())), preferred_element_type=jnp.float32)
             s = s * (HEAD_DIM ** (-0.5))
             kpos = key_first + lax.broadcasted_iota(jnp.int32, (BLOCK, BLOCK), 1)
@@ -64,7 +68,7 @@
 
         @pl.when(needed[t])
         def _():
-            v = v_ref[pl.ds(pl.multiple_of(key_first, BLOCK), BLOCK), :]
+            v = v_refs[t][...]
             w = (s_scr[t] * l_scr[...]).astype(jnp.bfloat16)
             acc_scr[...] += jnp.dot(w, v, preferred_element_type=jnp.float32)
     o_ref[...] = acc_scr[...].astype(o_ref.dtype)
@@ -73,15 +77,20 @@
 def attend(rows, doc_start, doc_most):
     tokens = rows.shape[0]
     tiles = doc_most // BLOCK + 1
+    lead = doc_most // BLOCK
+
+    def key_tile(t, column):
+        return pl.BlockSpec((BLOCK, HEAD_DIM), lambda b, f: (jnp.maximum(b - lead, 0) + t, column))
+
     grid_spec = pltpu.PrefetchScalarGridSpec(
         num_scalar_prefetch=1,
         grid=(tokens // BLOCK,),
         in_specs=[
             pl.BlockSpec((BLOCK, HEAD_DIM), lambda b, f: (b, 0)),
-            pl.BlockSpec((tokens, HEAD_DIM), lambda b, f: (0, 1)),
-            pl.BlockSpec((tokens, HEAD_DIM), lambda b, f: (0, 2)),
-            pl.BlockSpec((BLOCK, 1), lambda b, f: (b, 0)),
-        ],
+        ]
+        + [key_tile(t, 1) for t in range(tiles)]
+        + [key_tile(t, 2) for t in range(tiles)]
+        + [pl.BlockSpec((BLOCK, 1), lambda b, f: (b, 0))],
         out_specs=pl.BlockSpec((BLOCK, HEAD_DIM), lambda b, f: (b, 0)),
         scratch_shapes=[
             pltpu.VMEM((tiles, BLOCK, BLOCK), jnp.float32),
@@ -95,7 +104,7 @@
         functools.partial(attn_kernel, doc_most),
         grid_spec=grid_spec,
         out_shape=jax.ShapeDtypeStruct((tokens, HEAD_DIM), jnp.bfloat16),
-    )(block_firsts, rows, rows, rows, doc_start.reshape(tokens, 1))
+    )(block_firsts, *([rows] * (1 + 2 * tiles)), doc_start.reshape(tokens, 1))
 
 
 def per_device(queries, keys, values, order, doc_lengths):

time: 322 us -> 323 us (level)
  the two profiles are of different devices: /device:TPU:43 before, /device:TPU:6 now
where the time goes in v3:
time: 323 us; the launch traced here: 320 us
  blocking collectives  93.2 us (29%)
  local copies, waits for them, and re-layouts  76.6 us (24%)
  waiting for transfers between devices  73.4 us (23%)
  Pallas kernels  44.1 us (14%)
  between operations  13.5 us (4%)
  other arithmetic  10.9 us (3%)
  starting transfers between devices  8.42 us (3%)
    all_to_all x1, blocking collectives, per_device(): lax.all_to_all(slotted, ('z', 'y'), split_axis=0, concat_axis=1, tiled=True)  65.5 us
    all_to_all x1, waiting for transfers between devices, per_device(): lax.all_to_all(query_split, ('z', 'y'), split_axis=1, concat_axis=0, tile...  61.2 us
    pallas_call x1, Pallas kernels, attend(): pl.pallas_call(functools.partial(attn_kernel, doc_most), grid_spec=grid_s...  44.1 us
    gather x1, local copies, waits for them, and re-layouts, per_device(): joined.at[ring_row].get(mode='promise_in_bounds', unique_indices=True)  36 us
    all_to_all x1, blocking collectives, per_device(): lax.all_to_all(paired, 'z', split_axis=1, concat_axis=0, tiled=True)  27.7 us
    gather x1, local copies, waits for them, and re-layouts, per_device(): context.at[order].get(mode='promise_in_bounds', unique_indices=True)  23.8 us
    all_gather x1, waiting for transfers between devices, per_device(): lax.all_gather(kv_col, 'y', axis=0, tiled=True)  12.3 us
    all_to_all x1, starting transfers between devices, per_device(): lax.all_to_all(query_split, ('z', 'y'), split_axis=1, concat_axis=0, tile...  8.42 us
  transfers between devices with their start and end apart: 2, of which 2 were waited for; matrix products, arithmetic and copies ran while one was open for 5% of the time, Pallas kernels for 0%

profile of v3, /device:TPU:6, one launch (start us, length us, event | category | flops | bytes accessed | tf_op | source)
XLA Modules:
  0.0 320.2 jit_solution(4693374439053430703)
XLA Ops:
  6.5 0.0 all-gather.2.cloned.1.call-start
  6.5 1.1 copy.43
  7.7 1.1 copy.42
  8.8 0.1 pad_maximum_fusion.1
  8.8 0.3 copy.44
  9.1 0.0 copy-start.1
  9.1 27.7 %all_to_all.52 = bf16[128,8,2,128]{3,0,2,1:T(8,128)(2,1)S(1)} all-to-all(bf16[128,8,2,128]{3,0,2,1:T(8,128)(2,1)S(1)} %copy.44), channel_id=1, replica_groups=mesh['dp'=8,'z'=8,'y'=8] {'z'}, dimensions={1} | all-to-all | bytes 1048576 | tf_op jit(solution)/shard_map/all_to_all | solution.py:123
  36.9 1.3 copy.46
  38.3 0.0 all-gather.2.cloned.1.call-update
  38.3 0.0 copy-done.1
  38.3 2.4 copy.39
  40.7 0.0 copy-start.3
  40.7 8.4 %all-to-all-start = ((bf16[128,64,128]{0,2,1:T(8,128)(2,1)}), bf16[128,64,128]{0,2,1:T(8,128)(2,1)S(1)}, u32[]{:S(2)}, u32[]{:S(2)}) async-start(bf16[128,64,128]{0,2,1:T(8,128)(2,1)} %bitcast.33), calls=%async_computation | async-start | bytes 4194304 | tf_op jit(solution)/shard_map/all_to_all | solution.py:116
  49.2 0.0 copy-done.3
  49.2 0.1 copy.38
  49.3 0.1 reduce
  49.4 0.2 convert_reduce_fusion
  49.6 0.2 select_reduce_fusion
  49.8 0.0 copy-start.2
  49.8 2.7 copy.47.refs_7_
  52.5 0.0 copy-done.2
  52.5 6.8 %sort.15 = (s32[8192]{0:T(1024)}, s32[8192]{0:T(1024)S(1)}) sort(s32[8192]{0:T(1024)S(1)} %copy-done.2, s32[8192]{0:T(1024)S(1)} %iota.11), dimensions={0}, to_apply=%region_3.4 | sort | flops 106496 | bytes 131072 | tf_op jit(solution)/shard_map/sort | solution.py:128
  59.2 0.6 slice_reduce_fusion.first_ref
  59.9 0.1 fusion.4
  60.0 61.2 %all-to-all-done = bf16[128,64,128]{0,2,1:T(8,128)(2,1)S(1)} async-done(((bf16[128,64,128]{0,2,1:T(8,128)(2,1)}), bf16[128,64,128]{0,2,1:T(8,128)(2,1)S(1)}, u32[]{:S(2)}, u32[]{:S(2)}) %all-to-all-start) | async-done | bytes 2097184 | tf_op jit(solution)/shard_map/all_to_all | solution.py:116
  121.1 2.6 copy.41
  123.7 12.3 %all-gather.2.cloned.1.call-done = bf16[8192,1,2,128]{3,2,1,0:T(2,128)(2,1)} async-done(((bf16[1024,1,2,128]{3,2,1,0:T(2,128)(2,1)}), bf16[8192,1,2,128]{3,2,1,0:T(2,128)(2,1)}) %all-gather.2.cloned.1.call-update) | async-done | bytes 4194320 | tf_op jit(solution)/shard_map/all_gather | solution.py:124
  136.0 0.0 copy-start
  136.0 2.9 copy.54
  138.8 0.0 copy-done
  138.9 3.5 %pad_maximum_fusion = bf16[8192,384]{1,0:T(8,128)(2,1)} fusion(bf16[8192,256]{1,0:T(8,128)(2,1)S(1)} %bitcast.30, bf16[8192,128]{1,0:T(8,128)(2,1)S(1)} %bitcast.34), kind=kLoop, calls=%fused_computation.2 | loop fusion | flops 12582912 | bytes 12582912 | tf_op jit(solution)/shard_map/concatenate | solution.py:125
  142.3 36.0 %gather_fusion = bf16[8192,384]{1,0:T(8,128)(2,1)} fusion(bf16[8192,384]{1,0:T(8,128)(2,1)} %pad_maximum_fusion, s32[8192]{0:T(1024)S(1)} %fusion.4), kind=kCustom, calls=%fused_computation | custom fusion | bytes 12615680 | tf_op jit(solution)/shard_map/gather | solution.py:131
  178.3 44.1 %shard_map.55 = bf16[8192,128]{1,0:T(8,128)(2,1)} custom-call(s32[16]{0:T(128)} %slice_reduce_fusion.first_ref, bf16[8192,384]{1,0:T(8,128)(2,1)} %gather_fusion, bf16[8192,384]{1,0:T(8,128)(2,1)} %gather_fusion, bf16[8192,384]{1,0:T(8,128)(2,1)} %gather_fusion, bf16[8192,384]{1,0:T(8,128)(2,1)} %gather_fusion, bf16[8192,384]{1,0:T(8,128)(2,1)} %gather_fusion, ...), custom_call_target="tpu_custom_call" | custom-call | tf_op jit(solution)/shard_map/pallas_call | solution.py:103
  222.5 23.8 %gather_fusion.1 = bf16[8192,128]{1,0:T(8,128)(2,1)S(1)} fusion(bf16[8192,128]{1,0:T(8,128)(2,1)} %shard_map.55, s32[8192]{0:T(1024)S(1)} %fusion.5), kind=kCustom, calls=%fused_computation.1 | custom fusion | bytes 4227072 | tf_op jit(solution)/shard_map/gather | solution.py:134
  246.2 65.5 %all_to_all.53 = bf16[64,128,128]{2,1,0:T(8,128)(2,1)S(1)} all-to-all(bf16[64,128,128]{2,1,0:T(8,128)(2,1)S(1)} %bitcast.31), channel_id=1, replica_groups=mesh['dp'=8,'z'=8,'y'=8] {'z','y'}, dimensions={0} | all-to-all | bytes 4194304 | tf_op jit(solution)/shard_map/all_to_all | solution.py:135
  311.7 1.6 copy_bitcast_fusion.1
  (6 shorter events, 0.1 us)
Async XLA Ops:
  6.5 129.4 %all-gather.2.cloned.1.call-start = ((), (), s32[]{:S(2)}) async-start(), calls=%async_computation.3 | async-start | bytes 4718592 | tf_op jit(solution)/shard_map/all_gather | solution.py:124
  9.1 29.2 %copy-start.1 = (bf16[128,8192]{1,0:T(8,128)(2,1)S(1)}, bf16[128,8192]{1,0:T(8,128)(2,1)}, u32[]{:S(2)}) copy-start(bf16[128,8192]{1,0:T(8,128)(2,1)} %param.5) | copy-start | bytes 6291460
  40.7 8.4 %copy-start.3 = (s32[16]{0:T(128)S(1)}, s32[16]{0:T(128)}, u32[]{:S(2)}) copy-start(s32[16]{0:T(128)} %param.9) | copy-start | bytes 196
  40.7 80.4 %all-to-all-start = ((bf16[128,64,128]{0,2,1:T(8,128)(2,1)}), bf16[128,64,128]{0,2,1:T(8,128)(2,1)S(1)}, u32[]{:S(2)}, u32[]{:S(2)}) async-start(bf16[128,64,128]{0,2,1:T(8,128)(2,1)} %bitcast.33), calls=%async_computation | async-start | bytes 4194304 | tf_op jit(solution)/shard_map/all_to_all | solution.py:116
  49.8 2.7 copy-start.2
  136.0 2.9 copy-start
Sparse Core Ops, SparseCore 0:
  38.4 97.5 all-gather.1

commit v4 on v1

--- a/solution.py
+++ b/solution.py
@@ -24,7 +24,7 @@
     return jnp.sum(jnp.where(matches, doc_firsts[None, :], 0), axis=1)
 
 
-def attn_kernel(doc_most, first_ref, q_ref, k_ref, v_ref, ds_ref, o_ref, s_scr, m_scr, l_scr, acc_scr):
+def attn_kernel(doc_most, first_ref, q_ref, k_ref, v_ref, ds_ref, o_ref, m_scr, l_scr, acc_scr):
     b = pl.program_id(0)
     tiles = doc_most // BLOCK + 1
     start = pl.multiple_of(jnp.maximum(b * BLOCK - doc_most, 0), BLOCK)
@@ -33,7 +33,7 @@
     q = q_ref[...]
     qpos = q_first + lax.broadcasted_iota(jnp.int32, (BLOCK, BLOCK), 0)
     ds = ds_ref[...]
-    m_scr[...] = jnp.full(m_scr.shape, -jnp.inf, jnp.float32)
+    m_scr[...] = jnp.full(m_scr.shape, -1e30, jnp.float32)
     l_scr[...] = jnp.zeros(l_scr.shape, jnp.float32)
     acc_scr[...] = jnp.zeros(acc_scr.shape, jnp.float32)
     needed = []
@@ -46,26 +46,21 @@
         @pl.when(needed[t])
         def _():
             k = k_ref[pl.ds(pl.multiple_of(key_first, BLOCK), BLOCK), :]
+            v = v_ref[pl.ds(pl.multiple_of(key_first, BLOCK), BLOCK), :]
             s = lax.dot_general(q, k, (((1,), (1,)), ((), ())), preferred_element_type=jnp.float32)
             s = s * (HEAD_DIM ** (-0.5))
             kpos = key_first + lax.broadcasted_iota(jnp.int32, (BLOCK, BLOCK), 1)
             s = jnp.where((kpos <= qpos) & (kpos >= ds), s, -jnp.inf)
-            s_scr[t] = s
-            m_scr[...] = jnp.maximum(m_scr[...], jnp.max(s, axis=1, keepdims=True))
-    for t in range(tiles):
-        @pl.when(needed[t])
-        def _():
-            e = jnp.exp(s_scr[t] - m_scr[...])
-            s_scr[t] = e
-            l_scr[...] += jnp.sum(e, axis=1, keepdims=True)
-    for t in range(tiles):
-        key_first = start + t * BLOCK
-
-        @pl.when(needed[t])
-        def _():
-            v = v_ref[pl.ds(pl.multiple_of(key_first, BLOCK), BLOCK), :]
-            w = (s_scr[t] / l_scr[...]).astype(jnp.bfloat16)
-            acc_scr[...] += jnp.dot(w, v, preferred_element_type=jnp.float32)
+            m_old = m_scr[...]
+            m_new = jnp.maximum(m_old, jnp.max(s, axis=1, keepdims=True))
+            rescale = jnp.exp(m_old - m_new)
+            e = jnp.exp(s - m_new)
+            l_scr[...] = l_scr[...] * rescale + jnp.sum(e, axis=1, keepdims=True)
+            acc_scr[...] = acc_scr[...] * rescale + jnp.dot(
+                e.astype(jnp.bfloat16), v, preferred_element_type=jnp.float32
+            )
+            m_scr[...] = m_new
+    acc_scr[...] = acc_scr[...] * (1.0 / l_scr[...])
     o_ref[...] = acc_scr[...].astype(o_ref.dtype)
 
 
@@ -83,7 +78,6 @@
         ],
         out_specs=pl.BlockSpec((BLOCK, HEAD_DIM), lambda b, f: (b, 0)),
         scratch_shapes=[
-            pltpu.VMEM((tiles, BLOCK, BLOCK), jnp.float32),
             pltpu.VMEM((BLOCK, 1), jnp.float32),
             pltpu.VMEM((BLOCK, 1), jnp.float32),
             pltpu.VMEM((BLOCK, HEAD_DIM), jnp.float32),

time: 322 us -> 329 us (1.022)
  Pallas kernels: 43.8 us -> 53.2 us
    pallas_call x1, Pallas kernels: 43.8 us -> 53.2 us  [attend(): pl.pallas_call(functools.partial(attn_kernel, doc_most), grid_spec=grid_s...]
where the time goes in v4:
time: 329 us; the launch traced here: 326 us
  blocking collectives  89.9 us (27%)
  local copies, waits for them, and re-layouts  76.6 us (23%)
  waiting for transfers between devices  73.4 us (22%)
  Pallas kernels  53.2 us (16%)
  between operations  13.5 us (4%)
  other arithmetic  10.9 us (3%)
  starting transfers between devices  8.42 us (3%)
    all_to_all x1, blocking collectives, per_device(): lax.all_to_all(slotted, ('z', 'y'), split_axis=0, concat_axis=1, tiled=True)  62.1 us
    all_to_all x1, waiting for transfers between devices, per_device(): lax.all_to_all(query_split, ('z', 'y'), split_axis=1, concat_axis=0, tile...  61.2 us
    pallas_call x1, Pallas kernels, attend(): pl.pallas_call(functools.partial(attn_kernel, doc_most), grid_spec=grid_s...  53.2 us
    gather x1, local copies, waits for them, and re-layouts, per_device(): joined.at[ring_row].get(mode='promise_in_bounds', unique_indices=True)  36 us
    all_to_all x1, blocking collectives, per_device(): lax.all_to_all(paired, 'z', split_axis=1, concat_axis=0, tiled=True)  27.7 us
    gather x1, local copies, waits for them, and re-layouts, per_device(): context.at[order].get(mode='promise_in_bounds', unique_indices=True)  23.8 us
    all_gather x1, waiting for transfers between devices, per_device(): lax.all_gather(kv_col, 'y', axis=0, tiled=True)  12.3 us
    all_to_all x1, starting transfers between devices, per_device(): lax.all_to_all(query_split, ('z', 'y'), split_axis=1, concat_axis=0, tile...  8.42 us
  transfers between devices with their start and end apart: 2, of which 2 were waited for; matrix products, arithmetic and copies ran while one was open for 5% of the time, Pallas kernels for 0%

profile of v4, /device:TPU:6, one launch (start us, length us, event | category | flops | bytes accessed | tf_op | source)
XLA Modules:
  0.0 325.9 jit_solution(13337592369174674173)
XLA Ops:
  6.5 0.0 all-gather.2.cloned.1.call-start
  6.5 1.1 copy.43
  7.7 1.1 copy.42
  8.8 0.1 pad_maximum_fusion.1
  8.8 0.3 copy.44
  9.1 0.0 copy-start.1
  9.1 27.7 %all_to_all.52 = bf16[128,8,2,128]{3,0,2,1:T(8,128)(2,1)S(1)} all-to-all(bf16[128,8,2,128]{3,0,2,1:T(8,128)(2,1)S(1)} %copy.44), channel_id=1, replica_groups=mesh['dp'=8,'z'=8,'y'=8] {'z'}, dimensions={1} | all-to-all | bytes 1048576 | tf_op jit(solution)/shard_map/all_to_all | solution.py:107
  36.9 1.3 copy.46
  38.3 0.0 all-gather.2.cloned.1.call-update
  38.3 0.0 copy-done.1
  38.3 2.4 copy.39
  40.7 0.0 copy-start.3
  40.7 8.4 %all-to-all-start = ((bf16[128,64,128]{0,2,1:T(8,128)(2,1)}), bf16[128,64,128]{0,2,1:T(8,128)(2,1)S(1)}, u32[]{:S(2)}, u32[]{:S(2)}) async-start(bf16[128,64,128]{0,2,1:T(8,128)(2,1)} %bitcast.33), calls=%async_computation | async-start | bytes 4194304 | tf_op jit(solution)/shard_map/all_to_all | solution.py:100
  49.2 0.0 copy-done.3
  49.2 0.1 copy.38
  49.3 0.1 reduce
  49.4 0.2 convert_reduce_fusion
  49.6 0.2 select_reduce_fusion
  49.8 0.0 copy-start.2
  49.8 2.7 copy.47.ds_ref
  52.5 0.0 copy-done.2
  52.5 6.8 %sort.15 = (s32[8192]{0:T(1024)}, s32[8192]{0:T(1024)S(1)}) sort(s32[8192]{0:T(1024)S(1)} %copy-done.2, s32[8192]{0:T(1024)S(1)} %iota.11), dimensions={0}, to_apply=%region_3.4 | sort | flops 106496 | bytes 131072 | tf_op jit(solution)/shard_map/sort | solution.py:112
  59.2 0.6 slice_reduce_fusion.first_ref
  59.9 0.1 fusion.4
  60.0 61.2 %all-to-all-done = bf16[128,64,128]{0,2,1:T(8,128)(2,1)S(1)} async-done(((bf16[128,64,128]{0,2,1:T(8,128)(2,1)}), bf16[128,64,128]{0,2,1:T(8,128)(2,1)S(1)}, u32[]{:S(2)}, u32[]{:S(2)}) %all-to-all-start) | async-done | bytes 2097184 | tf_op jit(solution)/shard_map/all_to_all | solution.py:100
  121.1 2.6 copy.41
  123.7 12.3 %all-gather.2.cloned.1.call-done = bf16[8192,1,2,128]{3,2,1,0:T(2,128)(2,1)} async-done(((bf16[1024,1,2,128]{3,2,1,0:T(2,128)(2,1)}), bf16[8192,1,2,128]{3,2,1,0:T(2,128)(2,1)}) %all-gather.2.cloned.1.call-update) | async-done | bytes 4194320 | tf_op jit(solution)/shard_map/all_gather | solution.py:108
  136.0 0.0 copy-start
  136.0 2.9 copy.54
  138.8 0.0 copy-done
  138.9 3.5 %pad_maximum_fusion = bf16[8192,384]{1,0:T(8,128)(2,1)} fusion(bf16[8192,256]{1,0:T(8,128)(2,1)S(1)} %bitcast.30, bf16[8192,128]{1,0:T(8,128)(2,1)S(1)} %bitcast.34), kind=kLoop, calls=%fused_computation.2 | loop fusion | flops 12582912 | bytes 12582912 | tf_op jit(solution)/shard_map/concatenate | solution.py:109
  142.3 36.0 %gather_fusion = bf16[8192,384]{1,0:T(8,128)(2,1)} fusion(bf16[8192,384]{1,0:T(8,128)(2,1)} %pad_maximum_fusion, s32[8192]{0:T(1024)S(1)} %fusion.4), kind=kCustom, calls=%fused_computation | custom fusion | bytes 12615680 | tf_op jit(solution)/shard_map/gather | solution.py:115
  178.3 53.2 %shard_map.55 = bf16[8192,128]{1,0:T(8,128)(2,1)} custom-call(s32[16]{0:T(128)} %slice_reduce_fusion.first_ref, bf16[8192,384]{1,0:T(8,128)(2,1)} %gather_fusion, bf16[8192,384]{1,0:T(8,128)(2,1)} %gather_fusion, bf16[8192,384]{1,0:T(8,128)(2,1)} %gather_fusion, s32[8192,1]{1,0:T(8,128)} %copy.47.ds_ref), custom_call_target="tpu_custom_call" | custom-call | tf_op jit(solution)/shard_map/pallas_call | solution.py:87
  231.6 23.8 %gather_fusion.1 = bf16[8192,128]{1,0:T(8,128)(2,1)S(1)} fusion(bf16[8192,128]{1,0:T(8,128)(2,1)} %shard_map.55, s32[8192]{0:T(1024)S(1)} %fusion.5), kind=kCustom, calls=%fused_computation.1 | custom fusion | bytes 4227072 | tf_op jit(solution)/shard_map/gather | solution.py:118
  255.3 62.1 %all_to_all.53 = bf16[64,128,128]{2,1,0:T(8,128)(2,1)S(1)} all-to-all(bf16[64,128,128]{2,1,0:T(8,128)(2,1)S(1)} %bitcast.31), channel_id=1, replica_groups=mesh['dp'=8,'z'=8,'y'=8] {'z','y'}, dimensions={0} | all-to-all | bytes 4194304 | tf_op jit(solution)/shard_map/all_to_all | solution.py:119
  317.4 1.6 copy_bitcast_fusion.1
  (6 shorter events, 0.1 us)
Async XLA Ops:
  6.5 129.4 %all-gather.2.cloned.1.call-start = ((), (), s32[]{:S(2)}) async-start(), calls=%async_computation.3 | async-start | bytes 4718592 | tf_op jit(solution)/shard_map/all_gather | solution.py:108
  9.1 29.2 %copy-start.1 = (bf16[128,8192]{1,0:T(8,128)(2,1)S(1)}, bf16[128,8192]{1,0:T(8,128)(2,1)}, u32[]{:S(2)}) copy-start(bf16[128,8192]{1,0:T(8,128)(2,1)} %param.5) | copy-start | bytes 6291460
  40.7 8.4 %copy-start.3 = (s32[16]{0:T(128)S(1)}, s32[16]{0:T(128)}, u32[]{:S(2)}) copy-start(s32[16]{0:T(128)} %param.9) | copy-start | bytes 196
  40.7 80.4 %all-to-all-start = ((bf16[128,64,128]{0,2,1:T(8,128)(2,1)}), bf16[128,64,128]{0,2,1:T(8,128)(2,1)S(1)}, u32[]{:S(2)}, u32[]{:S(2)}) async-start(bf16[128,64,128]{0,2,1:T(8,128)(2,1)} %bitcast.33), calls=%async_computation | async-start | bytes 4194304 | tf_op jit(solution)/shard_map/all_to_all | solution.py:100
  49.8 2.7 copy-start.2
  136.0 2.9 copy-start
Sparse Core Ops, SparseCore 0:
  38.4 97.5 all-gather.1

commit v5 on v2

--- a/solution.py
+++ b/solution.py
@@ -107,7 +107,7 @@
     query_heads = lax.all_to_all(query_split, ("z", "y"), split_axis=1, concat_axis=0, tiled=True)
     q_slots = query_heads.reshape(nz, ny, tok_rows, HEAD_DIM)
     q_ring = jnp.transpose(q_slots, (1, 0, 2, 3)).reshape(tokens, HEAD_DIM)
-    paired = jnp.stack(
+    paired = jnp.concatenate(
         [keys.reshape(tok_rows, KV_HEADS, HEAD_DIM), values.reshape(tok_rows, KV_HEADS, HEAD_DIM)],
         axis=2,
     )

time: 322 us -> 320 us (level)
  the two profiles are of different devices: /device:TPU:43 before, /device:TPU:6 now
where the time goes in v5:
time: 320 us; the launch traced here: 314 us
  blocking collectives  90.2 us (28%)
  waiting for transfers between devices  73.6 us (23%)
  local copies, waits for them, and re-layouts  71.8 us (22%)
  Pallas kernels  43.2 us (14%)
  other arithmetic  13.8 us (4%)
  between operations  13.5 us (4%)
  starting transfers between devices  8.24 us (3%)
    all_to_all x1, blocking collectives, per_device(): lax.all_to_all(slotted, ('z', 'y'), split_axis=0, concat_axis=1, tiled=True)  62.5 us
    all_to_all x1, waiting for transfers between devices, per_device(): lax.all_to_all(query_split, ('z', 'y'), split_axis=1, concat_axis=0, tile...  61.4 us
    pallas_call x1, Pallas kernels, attend(): pl.pallas_call(functools.partial(attn_kernel, doc_most), grid_spec=grid_s...  43.2 us
    gather x1, local copies, waits for them, and re-layouts, per_device(): joined.at[ring_row].get(mode='promise_in_bounds', unique_indices=True)  36 us
    all_to_all x1, blocking collectives, per_device(): lax.all_to_all(paired, 'z', split_axis=1, concat_axis=0, tiled=True)  27.7 us
    gather x1, local copies, waits for them, and re-layouts, per_device(): context.at[order].get(mode='promise_in_bounds', unique_indices=True)  23.8 us
    all_gather x1, waiting for transfers between devices, per_device(): lax.all_gather(kv_col, 'y', axis=0, tiled=True)  12.2 us
    all_to_all x1, starting transfers between devices, per_device(): lax.all_to_all(query_split, ('z', 'y'), split_axis=1, concat_axis=0, tile...  8.24 us
  transfers between devices with their start and end apart: 2, of which 2 were waited for; matrix products, arithmetic and copies ran while one was open for 5% of the time, Pallas kernels for 0%

profile of v5, /device:TPU:6, one launch (start us, length us, event | category | flops | bytes accessed | tf_op | source)
XLA Modules:
  0.0 314.3 jit_solution(11997078088634084983)
XLA Ops:
  6.5 0.0 copy-start
  6.5 0.0 copy-start.1
  6.5 0.0 all-gather.2.cloned.1.call-start
  6.5 0.9 copy-done
  7.5 1.1 copy_bitcast_fusion.1
  8.6 0.1 pad_maximum_fusion.1
  8.6 27.7 %all_to_all.52 = bf16[128,8,256]{2,0,1:T(8,128)(2,1)} all-to-all(bf16[128,8,256]{2,0,1:T(8,128)(2,1)S(1)} %pad_maximum_fusion.1), channel_id=1, replica_groups=mesh['dp'=8,'z'=8,'y'=8] {'z'}, dimensions={1} | all-to-all | bytes 1048576 | tf_op jit(solution)/shard_map/all_to_all | solution.py:114
  36.4 0.0 all-gather.2.cloned.1.call-update
  36.4 0.0 copy-done.1
  36.4 2.4 copy.25
  38.8 0.0 copy-start.3
  38.8 8.2 %all-to-all-start = ((bf16[128,64,128]{0,2,1:T(8,128)(2,1)}), bf16[128,64,128]{0,2,1:T(8,128)(2,1)S(1)}, u32[]{:S(2)}, u32[]{:S(2)}) async-start(bf16[128,64,128]{0,2,1:T(8,128)(2,1)} %bitcast.36), calls=%async_computation | async-start | bytes 4194304 | tf_op jit(solution)/shard_map/all_to_all | solution.py:107
  47.1 0.0 copy-done.3
  47.1 0.1 copy.24
  47.2 0.1 reduce
  47.3 0.2 convert_reduce_fusion
  47.5 0.2 select_reduce_fusion
  47.7 0.0 copy-start.2
  47.7 2.7 copy.30.ds_ref
  50.4 0.0 copy-done.2
  50.4 6.8 %sort.15 = (s32[8192]{0:T(1024)}, s32[8192]{0:T(1024)S(1)}) sort(s32[8192]{0:T(1024)S(1)} %copy-done.2, s32[8192]{0:T(1024)S(1)} %iota.11), dimensions={0}, to_apply=%region_3.4 | sort | flops 106496 | bytes 131072 | tf_op jit(solution)/shard_map/sort | solution.py:119
  57.1 0.6 slice_reduce_fusion.first_ref
  57.8 0.1 fusion.4
  57.9 61.4 %all-to-all-done = bf16[128,64,128]{0,2,1:T(8,128)(2,1)S(1)} async-done(((bf16[128,64,128]{0,2,1:T(8,128)(2,1)}), bf16[128,64,128]{0,2,1:T(8,128)(2,1)S(1)}, u32[]{:S(2)}, u32[]{:S(2)}) %all-to-all-start) | async-done | bytes 2097184 | tf_op jit(solution)/shard_map/all_to_all | solution.py:107
  119.2 2.6 copy.27
  121.8 12.2 %all-gather.2.cloned.1.call-done = bf16[8192,1,256]{2,0,1:T(8,128)(2,1)} async-done(((bf16[1024,1,256]{2,0,1:T(8,128)(2,1)}), bf16[8192,1,256]{2,0,1:T(8,128)(2,1)}) %all-gather.2.cloned.1.call-update) | async-done | bytes 4194320 | tf_op jit(solution)/shard_map/all_gather | solution.py:115
  134.0 6.3 %pad_maximum_fusion = bf16[8192,384]{1,0:T(8,128)(2,1)} fusion(bf16[8192,256]{1,0:T(8,128)(2,1)} %bitcast.38, bf16[8192,128]{1,0:T(8,128)(2,1)} %bitcast.37), kind=kLoop, calls=%fused_computation.2 | loop fusion | flops 12582912 | bytes 12582912 | tf_op jit(solution)/shard_map/concatenate | solution.py:116
  140.4 36.0 %gather_fusion = bf16[8192,384]{1,0:T(8,128)(2,1)} fusion(bf16[8192,384]{1,0:T(8,128)(2,1)} %pad_maximum_fusion, s32[8192]{0:T(1024)S(1)} %fusion.4), kind=kCustom, calls=%fused_computation | custom fusion | bytes 12615680 | tf_op jit(solution)/shard_map/gather | solution.py:122
  176.4 43.2 %shard_map.55 = bf16[8192,128]{1,0:T(8,128)(2,1)} custom-call(s32[16]{0:T(128)} %slice_reduce_fusion.first_ref, bf16[8192,384]{1,0:T(8,128)(2,1)} %gather_fusion, bf16[8192,384]{1,0:T(8,128)(2,1)} %gather_fusion, bf16[8192,384]{1,0:T(8,128)(2,1)} %gather_fusion, s32[8192,1]{1,0:T(8,128)} %copy.30.ds_ref), custom_call_target="tpu_custom_call" | custom-call | tf_op jit(solution)/shard_map/pallas_call | solution.py:94
  219.6 23.8 %gather_fusion.1 = bf16[8192,128]{1,0:T(8,128)(2,1)S(1)} fusion(bf16[8192,128]{1,0:T(8,128)(2,1)} %shard_map.55, s32[8192]{0:T(1024)S(1)} %fusion.5), kind=kCustom, calls=%fused_computation.1 | custom fusion | bytes 4227072 | tf_op jit(solution)/shard_map/gather | solution.py:125
  243.3 62.5 %all_to_all.53 = bf16[64,128,128]{2,1,0:T(8,128)(2,1)S(1)} all-to-all(bf16[64,128,128]{2,1,0:T(8,128)(2,1)S(1)} %bitcast.34), channel_id=1, replica_groups=mesh['dp'=8,'z'=8,'y'=8] {'z','y'}, dimensions={0} | all-to-all | bytes 4194304 | tf_op jit(solution)/shard_map/all_to_all | solution.py:126
  305.9 1.6 copy_bitcast_fusion
  (5 shorter events, 0.1 us)
Async XLA Ops:
  6.5 1.0 copy-start
  6.5 29.8 %copy-start.1 = (bf16[128,8192]{1,0:T(8,128)(2,1)S(1)}, bf16[128,8192]{1,0:T(8,128)(2,1)}, u32[]{:S(2)}) copy-start(bf16[128,8192]{1,0:T(8,128)(2,1)} %param.5) | copy-start | bytes 6291460
  6.5 127.5 %all-gather.2.cloned.1.call-start = ((), (), s32[]{:S(2)}) async-start(), calls=%async_computation.3 | async-start | bytes 4718592 | tf_op jit(solution)/shard_map/all_gather | solution.py:115
  38.8 8.3 %copy-start.3 = (s32[16]{0:T(128)S(1)}, s32[16]{0:T(128)}, u32[]{:S(2)}) copy-start(s32[16]{0:T(128)} %param.9) | copy-start | bytes 196
  38.8 80.4 %all-to-all-start = ((bf16[128,64,128]{0,2,1:T(8,128)(2,1)}), bf16[128,64,128]{0,2,1:T(8,128)(2,1)S(1)}, u32[]{:S(2)}, u32[]{:S(2)}) async-start(bf16[128,64,128]{0,2,1:T(8,128)(2,1)} %bitcast.36), calls=%async_computation | async-start | bytes 4194304 | tf_op jit(solution)/shard_map/all_to_all | solution.py:107
  47.7 2.7 copy-start.2
Sparse Core Ops, SparseCore 0:
  36.5 97.5 all-gather.1

commit v6 on v5

--- a/solution.py
+++ b/solution.py
@@ -113,7 +113,9 @@
     )
     kv_col = lax.all_to_all(paired, "z", split_axis=1, concat_axis=0, tiled=True)
     kv_ring = lax.all_gather(kv_col, "y", axis=0, tiled=True).reshape(tokens, 2 * HEAD_DIM)
-    joined = jnp.concatenate([q_ring, kv_ring], axis=1)
+    joined = jnp.zeros((tokens, 3 * HEAD_DIM), q_ring.dtype).at[:, :HEAD_DIM].set(q_ring)
+    joined = lax.optimization_barrier(joined)
+    joined = lax.dynamic_update_slice(joined, kv_ring, (0, HEAD_DIM))
     doc_most = tokens // 8
     slot_ids = jnp.arange(tokens, dtype=jnp.int32)
     _, slot_of = lax.sort((order, slot_ids), num_keys=1)

time: 320 us -> 320 us (level)
  the two profiles are of different devices: /device:TPU:6 before, /device:TPU:28 now
where the time goes in v6:
time: 320 us; the launch traced here: 319 us
  blocking collectives  97.4 us (30%)
  local copies, waits for them, and re-layouts  80.2 us (25%)
  waiting for transfers between devices  67 us (21%)
  Pallas kernels  43.2 us (14%)
  between operations  13.5 us (4%)
  other arithmetic  10 us (3%)
  starting transfers between devices  8.01 us (3%)
    all_to_all x1, blocking collectives, per_device(): lax.all_to_all(slotted, ('z', 'y'), split_axis=0, concat_axis=1, tiled=True)  69.7 us
    all_to_all x1, waiting for transfers between devices, per_device(): lax.all_to_all(query_split, ('z', 'y'), split_axis=1, concat_axis=0, tile...  59.5 us
    pallas_call x1, Pallas kernels, attend(): pl.pallas_call(functools.partial(attn_kernel, doc_most), grid_spec=grid_s...  43.2 us
    gather x1, local copies, waits for them, and re-layouts, per_device(): joined.at[ring_row].get(mode='promise_in_bounds', unique_indices=True)  36.1 us
    all_to_all x1, blocking collectives, per_device(): lax.all_to_all(paired, 'z', split_axis=1, concat_axis=0, tiled=True)  27.7 us
    gather x1, local copies, waits for them, and re-layouts, per_device(): context.at[order].get(mode='promise_in_bounds', unique_indices=True)  23.8 us
    all_to_all x1, starting transfers between devices, per_device(): lax.all_to_all(query_split, ('z', 'y'), split_axis=1, concat_axis=0, tile...  8.01 us
    all_gather x1, waiting for transfers between devices, per_device(): lax.all_gather(kv_col, 'y', axis=0, tiled=True)  7.49 us
  transfers between devices with their start and end apart: 2, of which 2 were waited for; matrix products, arithmetic and copies ran while one was open for 7% of the time, Pallas kernels for 0%

profile of v6, /device:TPU:28, one launch (start us, length us, event | category | flops | bytes accessed | tf_op | source)
XLA Modules:
  0.0 319.4 jit_solution(9281730063145641662)
XLA Ops:
  6.5 0.0 copy-start
  6.5 0.0 copy-start.1
  6.5 0.0 all-gather.2.cloned.1.call-start
  6.5 0.9 copy-done
  7.5 1.1 copy_bitcast_fusion.1
  8.6 0.1 pad_maximum_fusion
  8.6 27.7 %all_to_all.49 = bf16[128,8,256]{2,0,1:T(8,128)(2,1)} all-to-all(bf16[128,8,256]{2,0,1:T(8,128)(2,1)S(1)} %pad_maximum_fusion), channel_id=1, replica_groups=mesh['dp'=8,'z'=8,'y'=8] {'z'}, dimensions={1} | all-to-all | bytes 1048576 | tf_op jit(solution)/shard_map/all_to_all | solution.py:114
  36.4 0.0 all-gather.2.cloned.1.call-update
  36.4 0.0 copy-done.1
  36.4 2.4 copy.25
  38.8 0.0 copy-start.3
  38.8 8.0 %all-to-all-start = ((bf16[128,64,128]{0,2,1:T(8,128)(2,1)}), bf16[128,64,128]{0,2,1:T(8,128)(2,1)S(1)}, u32[]{:S(2)}, u32[]{:S(2)}) async-start(bf16[128,64,128]{0,2,1:T(8,128)(2,1)} %bitcast.36), calls=%async_computation | async-start | bytes 4194304 | tf_op jit(solution)/shard_map/all_to_all | solution.py:107
  46.8 0.0 copy-done.3
  46.9 0.1 copy.24
  47.0 0.1 reduce.7
  47.1 0.2 convert_reduce_fusion
  47.3 0.2 select_reduce_fusion
  47.5 0.0 copy-start.2
  47.5 2.7 copy.30.ds_ref
  50.2 0.0 copy-done.2
  50.2 6.8 %sort.15 = (s32[8192]{0:T(1024)}, s32[8192]{0:T(1024)S(1)}) sort(s32[8192]{0:T(1024)S(1)} %copy-done.2, s32[8192]{0:T(1024)S(1)} %iota.15), dimensions={0}, to_apply=%region_4.5 | sort | flops 106496 | bytes 131072 | tf_op jit(solution)/shard_map/sort | solution.py:121
  56.9 0.6 compare_reduce_fusion
  57.5 0.6 slice_reduce_fusion.first_ref
  58.2 0.1 fusion.4
  58.2 59.5 %all-to-all-done = bf16[128,64,128]{0,2,1:T(8,128)(2,1)S(1)} async-done(((bf16[128,64,128]{0,2,1:T(8,128)(2,1)}), bf16[128,64,128]{0,2,1:T(8,128)(2,1)S(1)}, u32[]{:S(2)}, u32[]{:S(2)}) %all-to-all-start) | async-done | bytes 2097184 | tf_op jit(solution)/shard_map/all_to_all | solution.py:107
  117.8 2.0 broadcast_select_fusion
  119.8 3.1 copy.27
  122.8 3.3 %scatter.4 = bf16[8192,384]{1,0:T(8,128)(2,1)} pad(bf16[8192,128]{1,0:T(8,128)(2,1)S(1)} %bitcast.38, bf16[]{:T(256)} %constant.77.clone.1), padding=0_0x0_256 | pad | bytes 8388610 | tf_op jit(solution)/shard_map/scatter | solution.py:116
  126.2 7.5 %all-gather.2.cloned.1.call-done = bf16[8192,1,256]{2,0,1:T(8,128)(2,1)} async-done(((bf16[1024,1,256]{2,0,1:T(8,128)(2,1)}), bf16[8192,1,256]{2,0,1:T(8,128)(2,1)}) %all-gather.2.cloned.1.call-update) | async-done | bytes 4194320 | tf_op jit(solution)/shard_map/all_gather | solution.py:115
  133.7 4.5 %bitcast_dynamic-update-slice_fusion = bf16[8192,384]{1,0:T(8,128)(2,1)} fusion(bf16[8192,384]{1,0:T(8,128)(2,1)} %scatter.4, bf16[8192,1,256]{2,0,1:T(8,128)(2,1)} %all-gather.2.cloned.1.call-done), kind=kLoop, calls=%fused_computation.2 | loop fusion | bytes 8388608 | tf_op jit(solution)/shard_map/dynamic_update_slice | solution.py:118
  138.1 36.1 %gather_fusion = bf16[8192,384]{1,0:T(8,128)(2,1)} fusion(bf16[8192,384]{1,0:T(8,128)(2,1)} %bitcast_dynamic-update-slice_fusion, s32[8192]{0:T(1024)S(1)} %fusion.4), kind=kCustom, calls=%fused_computation | custom fusion | bytes 12615680 | tf_op jit(solution)/shard_map/gather | solution.py:124
  174.2 43.2 %shard_map.55 = bf16[8192,128]{1,0:T(8,128)(2,1)} custom-call(s32[16]{0:T(128)} %slice_reduce_fusion.first_ref, bf16[8192,384]{1,0:T(8,128)(2,1)} %gather_fusion, bf16[8192,384]{1,0:T(8,128)(2,1)} %gather_fusion, bf16[8192,384]{1,0:T(8,128)(2,1)} %gather_fusion, s32[8192,1]{1,0:T(8,128)} %copy.30.ds_ref), custom_call_target="tpu_custom_call" | custom-call | tf_op jit(solution)/shard_map/pallas_call | solution.py:94
  217.4 23.8 %gather_fusion.1 = bf16[8192,128]{1,0:T(8,128)(2,1)S(1)} fusion(bf16[8192,128]{1,0:T(8,128)(2,1)} %shard_map.55, s32[8192]{0:T(1024)S(1)} %fusion.5), kind=kCustom, calls=%fused_computation.1 | custom fusion | bytes 4227072 | tf_op jit(solution)/shard_map/gather | solution.py:127
  241.2 69.7 %all_to_all.50 = bf16[64,128,128]{2,1,0:T(8,128)(2,1)S(1)} all-to-all(bf16[64,128,128]{2,1,0:T(8,128)(2,1)S(1)} %bitcast.35), channel_id=1, replica_groups=mesh['dp'=8,'z'=8,'y'=8] {'z','y'}, dimensions={0} | all-to-all | bytes 4194304 | tf_op jit(solution)/shard_map/all_to_all | solution.py:128
  310.9 1.6 copy_bitcast_fusion
  (5 shorter events, 0.1 us)
Async XLA Ops:
  6.5 1.0 copy-start
  6.5 29.8 %copy-start.1 = (bf16[128,8192]{1,0:T(8,128)(2,1)S(1)}, bf16[128,8192]{1,0:T(8,128)(2,1)}, u32[]{:S(2)}) copy-start(bf16[128,8192]{1,0:T(8,128)(2,1)} %param.7) | copy-start | bytes 6291460
  6.5 127.1 %all-gather.2.cloned.1.call-start = ((), (), s32[]{:S(2)}) async-start(), calls=%async_computation.3 | async-start | bytes 4718592 | tf_op jit(solution)/shard_map/all_gather | solution.py:115
  38.8 8.0 %copy-start.3 = (s32[16]{0:T(128)S(1)}, s32[16]{0:T(128)}, u32[]{:S(2)}) copy-start(s32[16]{0:T(128)} %param.11) | copy-start | bytes 196
  38.8 78.9 %all-to-all-start = ((bf16[128,64,128]{0,2,1:T(8,128)(2,1)}), bf16[128,64,128]{0,2,1:T(8,128)(2,1)S(1)}, u32[]{:S(2)}, u32[]{:S(2)}) async-start(bf16[128,64,128]{0,2,1:T(8,128)(2,1)} %bitcast.36), calls=%async_computation | async-start | bytes 4194304 | tf_op jit(solution)/shard_map/all_to_all | solution.py:107
  47.5 2.7 copy-start.2
Sparse Core Ops, SparseCore 0:
  36.5 97.1 all-gather.1

commit v7 on v6

--- a/solution.py
+++ b/solution.py
@@ -31,7 +31,8 @@
     q_first = b * BLOCK
     ds_first = first_ref[b]
     q = q_ref[...]
-    qpos = q_first + lax.broadcasted_iota(jnp.int32, (BLOCK, BLOCK), 0)
+    row_pos = q_first + lax.broadcasted_iota(jnp.int32, (BLOCK, 1), 0)
+    col = lax.broadcasted_iota(jnp.int32, (BLOCK, BLOCK), 1)
     ds = ds_ref[...]
     m_scr[...] = jnp.full(m_scr.shape, -jnp.inf, jnp.float32)
     l_scr[...] = jnp.zeros(l_scr.shape, jnp.float32)
@@ -48,8 +49,7 @@
             k = k_ref[pl.ds(pl.multiple_of(key_first, BLOCK), BLOCK), :]
             s = lax.dot_general(q, k, (((1,), (1,)), ((), ())), preferred_element_type=jnp.float32)
             s = s * (HEAD_DIM ** (-0.5))
-            kpos = key_first + lax.broadcasted_iota(jnp.int32, (BLOCK, BLOCK), 1)
-            s = jnp.where((kpos <= qpos) & (kpos >= ds), s, -jnp.inf)
+            s = jnp.where((col <= row_pos - key_first) & (col >= ds - key_first), s, -jnp.inf)
             s_scr[t] = s
             m_scr[...] = jnp.maximum(m_scr[...], jnp.max(s, axis=1, keepdims=True))
     for t in range(tiles):

time: 320 us -> 318 us (level)
  the two profiles are of different devices: /device:TPU:28 before, /device:TPU:6 now
where the time goes in v7:
time: 318 us; the launch traced here: 317 us
  blocking collectives  89.9 us (28%)
  local copies, waits for them, and re-layouts  80.2 us (25%)
  waiting for transfers between devices  67.2 us (21%)
  Pallas kernels  48.1 us (15%)
  between operations  13.5 us (4%)
  other arithmetic  10 us (3%)
  starting transfers between devices  8.24 us (3%)
    all_to_all x1, blocking collectives, per_device(): lax.all_to_all(slotted, ('z', 'y'), split_axis=0, concat_axis=1, tiled=True)  62.2 us
    all_to_all x1, waiting for transfers between devices, per_device(): lax.all_to_all(query_split, ('z', 'y'), split_axis=1, concat_axis=0, tile...  60.8 us
    pallas_call x1, Pallas kernels, attend(): pl.pallas_call(functools.partial(attn_kernel, doc_most), grid_spec=grid_s...  48.1 us
    gather x1, local copies, waits for them, and re-layouts, per_device(): joined.at[ring_row].get(mode='promise_in_bounds', unique_indices=True)  36.1 us
    all_to_all x1, blocking collectives, per_device(): lax.all_to_all(paired, 'z', split_axis=1, concat_axis=0, tiled=True)  27.7 us
    gather x1, local copies, waits for them, and re-layouts, per_device(): context.at[order].get(mode='promise_in_bounds', unique_indices=True)  23.8 us
    all_to_all x1, starting transfers between devices, per_device(): lax.all_to_all(query_split, ('z', 'y'), split_axis=1, concat_axis=0, tile...  8.24 us
    sort x1, other arithmetic, per_device(): _, slot_of = lax.sort((order, slot_ids), num_keys=1)  6.75 us
  transfers between devices with their start and end apart: 2, of which 2 were waited for; matrix products, arithmetic and copies ran while one was open for 7% of the time, Pallas kernels for 0%

profile of v7, /device:TPU:6, one launch (start us, length us, event | category | flops | bytes accessed | tf_op | source)
XLA Modules:
  0.0 317.1 jit_solution(630012850794478129)
XLA Ops:
  6.5 0.0 copy-start
  6.5 0.0 copy-start.1
  6.5 0.0 all-gather.2.cloned.1.call-start
  6.5 0.9 copy-done
  7.5 1.1 copy_bitcast_fusion.1
  8.6 0.1 pad_maximum_fusion
  8.6 27.7 %all_to_all.49 = bf16[128,8,256]{2,0,1:T(8,128)(2,1)} all-to-all(bf16[128,8,256]{2,0,1:T(8,128)(2,1)S(1)} %pad_maximum_fusion), channel_id=1, replica_groups=mesh['dp'=8,'z'=8,'y'=8] {'z'}, dimensions={1} | all-to-all | bytes 1048576 | tf_op jit(solution)/shard_map/all_to_all | solution.py:114
  36.4 0.0 all-gather.2.cloned.1.call-update
  36.4 0.0 copy-done.1
  36.4 2.4 copy.25
  38.8 0.0 copy-start.3
  38.8 8.2 %all-to-all-start = ((bf16[128,64,128]{0,2,1:T(8,128)(2,1)}), bf16[128,64,128]{0,2,1:T(8,128)(2,1)S(1)}, u32[]{:S(2)}, u32[]{:S(2)}) async-start(bf16[128,64,128]{0,2,1:T(8,128)(2,1)} %bitcast.36), calls=%async_computation | async-start | bytes 4194304 | tf_op jit(solution)/shard_map/all_to_all | solution.py:107
  47.1 0.0 copy-done.3
  47.1 0.1 copy.24
  47.2 0.1 reduce.7
  47.3 0.2 convert_reduce_fusion
  47.5 0.2 select_reduce_fusion
  47.7 0.0 copy-start.2
  47.7 2.7 copy.30.ds_ref
  50.4 0.0 copy-done.2
  50.4 6.8 %sort.15 = (s32[8192]{0:T(1024)}, s32[8192]{0:T(1024)S(1)}) sort(s32[8192]{0:T(1024)S(1)} %copy-done.2, s32[8192]{0:T(1024)S(1)} %iota.15), dimensions={0}, to_apply=%region_4.5 | sort | flops 106496 | bytes 131072 | tf_op jit(solution)/shard_map/sort | solution.py:121
  57.1 0.6 compare_reduce_fusion
  57.8 0.6 slice_reduce_fusion.first_ref
  58.4 0.1 fusion.4
  58.5 60.8 %all-to-all-done = bf16[128,64,128]{0,2,1:T(8,128)(2,1)S(1)} async-done(((bf16[128,64,128]{0,2,1:T(8,128)(2,1)}), bf16[128,64,128]{0,2,1:T(8,128)(2,1)S(1)}, u32[]{:S(2)}, u32[]{:S(2)}) %all-to-all-start) | async-done | bytes 2097184 | tf_op jit(solution)/shard_map/all_to_all | solution.py:107
  119.2 2.0 broadcast_select_fusion
  121.2 3.1 copy.27
  124.3 3.3 %scatter.4 = bf16[8192,384]{1,0:T(8,128)(2,1)} pad(bf16[8192,128]{1,0:T(8,128)(2,1)S(1)} %bitcast.38, bf16[]{:T(256)} %constant.77.clone.1), padding=0_0x0_256 | pad | bytes 8388610 | tf_op jit(solution)/shard_map/scatter | solution.py:116
  127.6 6.4 %all-gather.2.cloned.1.call-done = bf16[8192,1,256]{2,0,1:T(8,128)(2,1)} async-done(((bf16[1024,1,256]{2,0,1:T(8,128)(2,1)}), bf16[8192,1,256]{2,0,1:T(8,128)(2,1)}) %all-gather.2.cloned.1.call-update) | async-done | bytes 4194320 | tf_op jit(solution)/shard_map/all_gather | solution.py:115
  134.0 4.5 %bitcast_dynamic-update-slice_fusion = bf16[8192,384]{1,0:T(8,128)(2,1)} fusion(bf16[8192,384]{1,0:T(8,128)(2,1)} %scatter.4, bf16[8192,1,256]{2,0,1:T(8,128)(2,1)} %all-gather.2.cloned.1.call-done), kind=kLoop, calls=%fused_computation.2 | loop fusion | bytes 8388608 | tf_op jit(solution)/shard_map/dynamic_update_slice | solution.py:118
  138.5 36.1 %gather_fusion = bf16[8192,384]{1,0:T(8,128)(2,1)} fusion(bf16[8192,384]{1,0:T(8,128)(2,1)} %bitcast_dynamic-update-slice_fusion, s32[8192]{0:T(1024)S(1)} %fusion.4), kind=kCustom, calls=%fused_computation | custom fusion | bytes 12615680 | tf_op jit(solution)/shard_map/gather | solution.py:124
  174.6 48.1 %shard_map.55 = bf16[8192,128]{1,0:T(8,128)(2,1)} custom-call(s32[16]{0:T(128)} %slice_reduce_fusion.first_ref, bf16[8192,384]{1,0:T(8,128)(2,1)} %gather_fusion, bf16[8192,384]{1,0:T(8,128)(2,1)} %gather_fusion, bf16[8192,384]{1,0:T(8,128)(2,1)} %gather_fusion, s32[8192,1]{1,0:T(8,128)} %copy.30.ds_ref), custom_call_target="tpu_custom_call" | custom-call | tf_op jit(solution)/shard_map/pallas_call | solution.py:94
  222.7 23.8 %gather_fusion.1 = bf16[8192,128]{1,0:T(8,128)(2,1)S(1)} fusion(bf16[8192,128]{1,0:T(8,128)(2,1)} %shard_map.55, s32[8192]{0:T(1024)S(1)} %fusion.5), kind=kCustom, calls=%fused_computation.1 | custom fusion | bytes 4227072 | tf_op jit(solution)/shard_map/gather | solution.py:127
  246.4 62.2 %all_to_all.50 = bf16[64,128,128]{2,1,0:T(8,128)(2,1)S(1)} all-to-all(bf16[64,128,128]{2,1,0:T(8,128)(2,1)S(1)} %bitcast.35), channel_id=1, replica_groups=mesh['dp'=8,'z'=8,'y'=8] {'z','y'}, dimensions={0} | all-to-all | bytes 4194304 | tf_op jit(solution)/shard_map/all_to_all | solution.py:128
  308.7 1.6 copy_bitcast_fusion
  (5 shorter events, 0.1 us)
Async XLA Ops:
  6.5 1.0 copy-start
  6.5 29.8 %copy-start.1 = (bf16[128,8192]{1,0:T(8,128)(2,1)S(1)}, bf16[128,8192]{1,0:T(8,128)(2,1)}, u32[]{:S(2)}) copy-start(bf16[128,8192]{1,0:T(8,128)(2,1)} %param.7) | copy-start | bytes 6291460
  6.5 127.5 %all-gather.2.cloned.1.call-start = ((), (), s32[]{:S(2)}) async-start(), calls=%async_computation.3 | async-start | bytes 4718592 | tf_op jit(solution)/shard_map/all_gather | solution.py:115
  38.8 8.3 %copy-start.3 = (s32[16]{0:T(128)S(1)}, s32[16]{0:T(128)}, u32[]{:S(2)}) copy-start(s32[16]{0:T(128)} %param.11) | copy-start | bytes 196
  38.8 80.4 %all-to-all-start = ((bf16[128,64,128]{0,2,1:T(8,128)(2,1)}), bf16[128,64,128]{0,2,1:T(8,128)(2,1)S(1)}, u32[]{:S(2)}, u32[]{:S(2)}) async-start(bf16[128,64,128]{0,2,1:T(8,128)(2,1)} %bitcast.36), calls=%async_computation | async-start | bytes 4194304 | tf_op jit(solution)/shard_map/all_to_all | solution.py:107
  47.7 2.7 copy-start.2
Sparse Core Ops, SparseCore 0:
  36.5 97.5 all-gather.1

commit v8 on v6

--- a/solution.py
+++ b/solution.py
@@ -107,15 +107,15 @@
     query_heads = lax.all_to_all(query_split, ("z", "y"), split_axis=1, concat_axis=0, tiled=True)
     q_slots = query_heads.reshape(nz, ny, tok_rows, HEAD_DIM)
     q_ring = jnp.transpose(q_slots, (1, 0, 2, 3)).reshape(tokens, HEAD_DIM)
-    paired = jnp.concatenate(
-        [keys.reshape(tok_rows, KV_HEADS, HEAD_DIM), values.reshape(tok_rows, KV_HEADS, HEAD_DIM)],
-        axis=2,
-    )
-    kv_col = lax.all_to_all(paired, "z", split_axis=1, concat_axis=0, tiled=True)
-    kv_ring = lax.all_gather(kv_col, "y", axis=0, tiled=True).reshape(tokens, 2 * HEAD_DIM)
+    rings = []
+    for part in (keys, values):
+        split = part.reshape(tok_rows, KV_HEADS, HEAD_DIM)
+        col = lax.all_to_all(split, "z", split_axis=1, concat_axis=0, tiled=True)
+        rings.append(lax.all_gather(col, "y", axis=0, tiled=True).reshape(tokens, HEAD_DIM))
     joined = jnp.zeros((tokens, 3 * HEAD_DIM), q_ring.dtype).at[:, :HEAD_DIM].set(q_ring)
     joined = lax.optimization_barrier(joined)
-    joined = lax.dynamic_update_slice(joined, kv_ring, (0, HEAD_DIM))
+    joined = lax.dynamic_update_slice(joined, rings[0], (0, HEAD_DIM))
+    joined = lax.dynamic_update_slice(joined, rings[1], (0, 2 * HEAD_DIM))
     doc_most = tokens // 8
     slot_ids = jnp.arange(tokens, dtype=jnp.int32)
     _, slot_of = lax.sort((order, slot_ids), num_keys=1)

time: 320 us -> 316 us (0.988)
  the two profiles are of different devices: /device:TPU:28 before, /device:TPU:6 now
where the time goes in v8:
time: 316 us; the launch traced here: 315 us
  local copies, waits for them, and re-layouts  83.3 us (26%)
  blocking collectives  82.7 us (26%)
  waiting for transfers between devices  70.2 us (22%)
  Pallas kernels  43.2 us (14%)
  between operations  13.5 us (4%)
  starting transfers between devices  11.6 us (4%)
  other arithmetic  9.97 us (3%)
    all_to_all x1, blocking collectives, per_device(): lax.all_to_all(slotted, ('z', 'y'), split_axis=0, concat_axis=1, tiled=True)  60.6 us
    all_to_all x1, waiting for transfers between devices, per_device(): lax.all_to_all(query_split, ('z', 'y'), split_axis=1, concat_axis=0, tile...  49.6 us
    pallas_call x1, Pallas kernels, attend(): pl.pallas_call(functools.partial(attn_kernel, doc_most), grid_spec=grid_s...  43.2 us
    gather x1, local copies, waits for them, and re-layouts, per_device(): joined.at[ring_row].get(mode='promise_in_bounds', unique_indices=True)  36.1 us
    gather x1, local copies, waits for them, and re-layouts, per_device(): context.at[order].get(mode='promise_in_bounds', unique_indices=True)  23.8 us
    all_to_all x1, blocking collectives, per_device(): col = lax.all_to_all(split, 'z', split_axis=1, concat_axis=0, tiled=True)  22.1 us
    all_gather x2, waiting for transfers between devices, per_device(): lax.all_gather(col, 'y', axis=0, tiled=True).reshape(tokens, HEAD_DIM)  12 us
    all_to_all x1, starting transfers between devices, per_device(): lax.all_to_all(query_split, ('z', 'y'), split_axis=1, concat_axis=0, tile...  8.17 us
  transfers between devices with their start and end apart: 4, of which 3 were waited for; matrix products, arithmetic and copies ran while one was open for 9% of the time, Pallas kernels for 0%

profile of v8, /device:TPU:6, one launch (start us, length us, event | category | flops | bytes accessed | tf_op | source)
XLA Modules:
  0.0 314.6 jit_solution(14681267950265487359)
XLA Ops:
  6.5 0.0 copy-start
  6.5 0.0 copy-start.1
  6.5 0.0 all-gather.3.cloned.1.call-start
  6.5 0.9 copy-done
  7.5 22.1 %all_to_all.67 = bf16[128,8,128]{2,0,1:T(8,128)(2,1)} all-to-all(bf16[128,8,128]{2,0,1:T(8,128)(2,1)S(1)} %copy_bitcast_fusion.2), channel_id=1, replica_groups=mesh['dp'=8,'z'=8,'y'=8] {'z'}, dimensions={1} | all-to-all | bytes 524288 | tf_op jit(solution)/shard_map/all_to_all | solution.py:113
  29.6 0.0 all-gather.3.cloned.1.call-update
  29.7 1.7 copy_bitcast_fusion.1
  31.4 3.4 %all-to-all-start.2 = ((bf16[128,8,128]{2,0,1:T(8,128)(2,1)}), bf16[128,8,128]{2,0,1:T(8,128)(2,1)S(1)}, u32[]{:S(2)}, u32[]{:S(2)}) async-start(bf16[128,8,128]{2,0,1:T(8,128)(2,1)} %copy_bitcast_fusion.1), calls=%async_computation.2 | async-start | bytes 524288 | tf_op jit(solution)/shard_map/all_to_all | solution.py:113
  34.8 0.0 copy-done.1
  34.8 2.4 copy.25
  37.2 8.0 %all-to-all-done.2 = bf16[128,8,128]{2,0,1:T(8,128)(2,1)S(1)} async-done(((bf16[128,8,128]{2,0,1:T(8,128)(2,1)}), bf16[128,8,128]{2,0,1:T(8,128)(2,1)S(1)}, u32[]{:S(2)}, u32[]{:S(2)}) %all-to-all-start.2) | async-done | bytes 262176 | tf_op jit(solution)/shard_map/all_to_all | solution.py:113
  45.2 0.0 copy-start.2
  45.2 0.0 copy-start.4
  45.2 0.7 copy-done.2
  45.9 8.2 %all-to-all-start = ((bf16[128,64,128]{0,2,1:T(8,128)(2,1)}), bf16[128,64,128]{0,2,1:T(8,128)(2,1)S(1)}, u32[]{:S(2)}, u32[]{:S(2)}) async-start(bf16[128,64,128]{0,2,1:T(8,128)(2,1)} %bitcast.1), calls=%async_computation | async-start | bytes 4194304 | tf_op jit(solution)/shard_map/all_to_all | solution.py:107
  54.1 0.0 all-gather.5.cloned.1.call-start
  54.1 0.7 all-gather.5.cloned.1.call-update
  54.8 0.0 copy-done.4
  54.9 0.1 copy.24
  55.0 0.1 reduce.7
  55.1 0.2 convert_reduce_fusion
  55.3 0.2 select_reduce_fusion
  55.5 0.0 copy-start.3
  55.5 2.7 copy.30.ds_ref
  58.2 0.0 copy-done.3
  58.2 6.8 %sort.15 = (s32[8192]{0:T(1024)}, s32[8192]{0:T(1024)S(1)}) sort(s32[8192]{0:T(1024)S(1)} %copy-done.3, s32[8192]{0:T(1024)S(1)} %iota.15), dimensions={0}, to_apply=%region_4.5 | sort | flops 106496 | bytes 131072 | tf_op jit(solution)/shard_map/sort | solution.py:121
  64.9 0.6 compare_reduce_fusion
  65.5 0.6 slice_reduce_fusion.first_ref
  66.2 0.1 fusion.4
  66.2 49.6 %all-to-all-done = bf16[128,64,128]{0,2,1:T(8,128)(2,1)S(1)} async-done(((bf16[128,64,128]{0,2,1:T(8,128)(2,1)}), bf16[128,64,128]{0,2,1:T(8,128)(2,1)S(1)}, u32[]{:S(2)}, u32[]{:S(2)}) %all-to-all-start) | async-done | bytes 2097184 | tf_op jit(solution)/shard_map/all_to_all | solution.py:107
  115.8 2.0 broadcast_select_fusion
  117.8 3.0 copy.27
  120.9 3.3 %scatter.4 = bf16[8192,384]{1,0:T(8,128)(2,1)} pad(bf16[8192,128]{1,0:T(8,128)(2,1)S(1)} %bitcast.44, bf16[]{:T(256)} %constant.78.clone.1), padding=0_0x0_256 | pad | bytes 8388610 | tf_op jit(solution)/shard_map/scatter | solution.py:115
  124.2 0.0 all-gather.3.cloned.1.call-done
  124.2 3.1 bitcast_dynamic-update-slice_fusion.1
  127.4 12.0 %all-gather.5.cloned.1.call-done = bf16[8192,1,128]{2,0,1:T(8,128)(2,1)} async-done(((bf16[1024,1,128]{2,0,1:T(8,128)(2,1)}), bf16[8192,1,128]{2,0,1:T(8,128)(2,1)}) %all-gather.5.cloned.1.call-update) | async-done | bytes 2097168 | tf_op jit(solution)/shard_map/all_gather | solution.py:114
  139.3 3.1 bitcast_dynamic-update-slice_fusion
  142.5 36.1 %gather_fusion = bf16[8192,384]{1,0:T(8,128)(2,1)} fusion(bf16[8192,384]{1,0:T(8,128)(2,1)} %bitcast_dynamic-update-slice_fusion, s32[8192]{0:T(1024)S(1)} %fusion.4), kind=kCustom, calls=%fused_computation | custom fusion | bytes 12615680 | tf_op jit(solution)/shard_map/gather | solution.py:124
  178.5 43.2 %shard_map.55 = bf16[8192,128]{1,0:T(8,128)(2,1)} custom-call(s32[16]{0:T(128)} %slice_reduce_fusion.first_ref, bf16[8192,384]{1,0:T(8,128)(2,1)} %gather_fusion, bf16[8192,384]{1,0:T(8,128)(2,1)} %gather_fusion, bf16[8192,384]{1,0:T(8,128)(2,1)} %gather_fusion, s32[8192,1]{1,0:T(8,128)} %copy.30.ds_ref), custom_call_target="tpu_custom_call" | custom-call | tf_op jit(solution)/shard_map/pallas_call | solution.py:94
  221.7 23.8 %gather_fusion.1 = bf16[8192,128]{1,0:T(8,128)(2,1)S(1)} fusion(bf16[8192,128]{1,0:T(8,128)(2,1)} %shard_map.55, s32[8192]{0:T(1024)S(1)} %fusion.5), kind=kCustom, calls=%fused_computation.1 | custom fusion | bytes 4227072 | tf_op jit(solution)/shard_map/gather | solution.py:127
  245.5 60.6 %all_to_all.68 = bf16[64,128,128]{2,1,0:T(8,128)(2,1)S(1)} all-to-all(bf16[64,128,128]{2,1,0:T(8,128)(2,1)S(1)} %bitcast.42), channel_id=1, replica_groups=mesh['dp'=8,'z'=8,'y'=8] {'z','y'}, dimensions={0} | all-to-all | bytes 4194304 | tf_op jit(solution)/shard_map/all_to_all | solution.py:128
  306.1 1.6 copy_bitcast_fusion
  (6 shorter events, 0.1 us)
Async XLA Ops:
  6.5 1.0 copy-start
  6.5 28.2 %copy-start.1 = (bf16[128,8192]{1,0:T(8,128)(2,1)S(1)}, bf16[128,8192]{1,0:T(8,128)(2,1)}, u32[]{:S(2)}) copy-start(bf16[128,8192]{1,0:T(8,128)(2,1)} %param.7) | copy-start | bytes 6291460
  6.5 117.7 %all-gather.3.cloned.1.call-start = ((), (), s32[]{:S(2)}) async-start(), calls=%async_computation.4 | async-start | bytes 2359296 | tf_op jit(solution)/shard_map/all_gather | solution.py:114
  31.4 13.8 %all-to-all-start.2 = ((bf16[128,8,128]{2,0,1:T(8,128)(2,1)}), bf16[128,8,128]{2,0,1:T(8,128)(2,1)S(1)}, u32[]{:S(2)}, u32[]{:S(2)}) async-start(bf16[128,8,128]{2,0,1:T(8,128)(2,1)} %copy_bitcast_fusion.1), calls=%async_computation.2 | async-start | bytes 524288 | tf_op jit(solution)/shard_map/all_to_all | solution.py:113
  45.2 0.7 copy-start.2
  45.2 9.6 %copy-start.4 = (s32[16]{0:T(128)S(1)}, s32[16]{0:T(128)}, u32[]{:S(2)}) copy-start(s32[16]{0:T(128)} %param.11) | copy-start | bytes 196
  45.9 69.9 %all-to-all-start = ((bf16[128,64,128]{0,2,1:T(8,128)(2,1)}), bf16[128,64,128]{0,2,1:T(8,128)(2,1)S(1)}, u32[]{:S(2)}, u32[]{:S(2)}) async-start(bf16[128,64,128]{0,2,1:T(8,128)(2,1)} %bitcast.1), calls=%async_computation | async-start | bytes 4194304 | tf_op jit(solution)/shard_map/all_to_all | solution.py:107
  54.1 85.2 %all-gather.5.cloned.1.call-start = ((), (), s32[]{:S(2)}) async-start(), calls=%async_computation.5 | async-start | bytes 2359296 | tf_op jit(solution)/shard_map/all_gather | solution.py:114
  55.5 2.7 copy-start.3
Sparse Core Ops, SparseCore 0:
  29.8 63.0 all-gather.2
  95.0 44.3 all-gather.4
